TPU v7x, 128 devices: a whole 4x4x4 slice. The times are simulated.
128 devices in a mesh: rows: 32 (over z, x, core), sk: 4 (over y).
Axes of the slice: x: 4, y: 4, z: 4, core: 2. Of those that a mesh axis runs over, the one named last changes fastest.
Arguments:
- panel: float32 [64, 1048576], P(None, ('rows', 'sk')), may hold values from -200 to 200
- signs: int32 [1048576], P(('rows', 'sk')), may hold values from -1 to 1
- sample_device: int32 [16384, 1], replicated, may hold values from 0 to 127; in each aligned block of 128 rows (0 to 127, 128 to 255, ...) at most 4 rows name the same one
- sample_offset: int32 [16384], replicated, may hold values from 0 to 8191
Outputs:
- mixed: float32 [64, 1048576], P(None, ('rows', 'sk'))
- r_factor: float32 [64, 64], replicated
- whitened: float32 [64, 16384], P(None, ('rows', 'sk'))
Inputs may be any that keep to these rules, and one draw needn't show every extreme that they name: `sample_device`: among the sample positions j * 128 to (j + 1) * 128 - 1 of any j, no device number appears more than 4 times, and some block reaches it.
All inputs are finite; a program needn't handle non-finite values.
Results may differ from a plain program's by a relative error of at most 0.0003.
Values sent between devices are 32-bit elements; how exact they have to be, the bound alone decides.
A program may use at most 64 MiB of HBM per device.

v0:
```python
import math

import jax
import jax.numpy as jnp
from jax import lax
from jax.sharding import PartitionSpec as P

CAP = 4


def grouped_exchange(array, axis, split_dim, concat_dim, work, item_dim, out_dim):

    def moved(group):
        return lax.all_to_all(group, axis, split_axis=split_dim, concat_axis=concat_dim, tiled=True)

    items = jax.tree.leaves(array)[0].shape[item_dim]
    ends = [items * k // 2 for k in range(2 + 1)] if items % 2 == 0 else [0, items]
    groups = [
        jax.tree.map(lambda a: lax.slice_in_dim(a, low, high, axis=item_dim), array)
        for low, high in zip(ends, ends[1:])
    ]
    arrived = [moved(group) for group in groups]
    made = [work(group) for group in arrived]
    return jax.tree.map(lambda *parts: jnp.concatenate(parts, axis=out_dim), *made)


def hadamard_table(order_size):
    left_ids = jnp.arange(order_size, dtype=jnp.int32)[:, None]
    right_ids = jnp.arange(order_size, dtype=jnp.int32)[None, :]
    common = jnp.bitwise_and(left_ids, right_ids)
    parity = jnp.zeros((order_size, order_size), jnp.int32)
    for bit_number in range(max(order_size.bit_length() - 1, 1)):
        parity = parity + jnp.bitwise_and(jnp.right_shift(common, bit_number), 1)
    return jnp.where(parity % 2 == 0, 1.0, -1.0).astype(jnp.float32)


def householder_r(matrix):
    rows_count, cols_count = matrix.shape
    position = jnp.arange(rows_count, dtype=jnp.int32)

    def reflect(j, current):
        column = lax.dynamic_slice_in_dim(current, j, 1, 1)[:, 0]
        column = jnp.where(position >= j, column, jnp.float32(0.0))
        pivot_value = column[j]
        length = jnp.sqrt(jnp.sum(column * column))
        signed = jnp.where(pivot_value >= 0, jnp.float32(1.0), jnp.float32(-1.0))
        vector = column + signed * length * (position == j).astype(jnp.float32)
        denominator = jnp.sum(vector * vector)
        projection = jnp.dot(vector, current, precision=lax.Precision.HIGHEST)
        return current - vector[:, None] * projection[None, :] * (2.0 / denominator)

    reduced = lax.fori_loop(0, cols_count, reflect, matrix)
    upper = jnp.triu(reduced[:cols_count])
    diag_signs = jnp.where(jnp.diagonal(upper) >= 0, jnp.float32(1.0), jnp.float32(-1.0))
    return upper * diag_signs[:, None]


def forward_solve(upper, values):
    lower = upper.T
    order_size = lower.shape[0]

    def step_row(i, solved):
        row_coef = lax.dynamic_slice_in_dim(lower, i, 1, 0)
        partial_sum = jnp.dot(row_coef, solved, precision=lax.Precision.HIGHEST)
        target = lax.dynamic_slice_in_dim(values, i, 1, 0)
        pivot = lax.dynamic_slice_in_dim(row_coef[0], i, 1, 0)
        new_row = (target - partial_sum) / pivot[0]
        return lax.dynamic_update_slice_in_dim(solved, new_row, i, 0)

    return lax.fori_loop(0, order_size, step_row, jnp.zeros(values.shape, jnp.float32))


def local(panel, signs, sample_device, sample_offset):
    high = lax.Precision.HIGHEST
    device_count = lax.axis_size(("rows", "sk"))
    device_id = lax.axis_index(("rows", "sk"))
    cols_here, local_rows = panel.shape
    inner = local_rows // 128
    flipped = panel * signs.astype(jnp.float32)[None, :]
    cube = flipped.reshape(cols_here, inner, 128)
    cube = jnp.einsum("cab,ea->ceb", cube, hadamard_table(inner), precision=high)
    cube = jnp.einsum("cab,db->cad", cube, hadamard_table(128), precision=high)
    local_mix = cube.reshape(cols_here, local_rows)
    piece_rows = local_rows // device_count
    device_table = hadamard_table(device_count)

    def combine_pieces(received):
        grouped = received.reshape(received.shape[0], device_count, piece_rows)
        mixed_pieces = jnp.einsum("cqr,pq->cpr", grouped, device_table, precision=high)
        flat_pieces = mixed_pieces.reshape(received.shape[0], local_rows)
        return lax.all_to_all(flat_pieces, ("rows", "sk"), split_axis=1, concat_axis=1, tiled=True)

    spread = grouped_exchange(local_mix, ("rows", "sk"), 1, 1, combine_pieces, 0, 0)
    mixed = spread * (1.0 / math.sqrt(local_rows * device_count))
    sources = sample_device[:, 0]
    total_samples = sources.shape[0]
    per_owner = total_samples // device_count
    mine = (sources == device_id).astype(jnp.int32).reshape(device_count, per_owner)
    rank_send = jnp.cumsum(mine, axis=1) - 1
    owner_ids = jnp.arange(device_count, dtype=jnp.int32)[:, None]
    slot_number = jnp.where(mine == 1, owner_ids * CAP + rank_send, device_count * CAP).reshape(-1)
    slot_offset = (
        jnp.zeros((device_count * CAP,), jnp.int32).at[slot_number].set(sample_offset, mode="drop")
    )
    slot_live = jnp.zeros((device_count * CAP,), jnp.float32).at[slot_number].set(1.0, mode="drop")
    outgoing = jnp.take(mixed, slot_offset, axis=1) * slot_live[None, :]
    incoming = lax.all_to_all(outgoing, ("rows", "sk"), split_axis=1, concat_axis=1, tiled=True)
    own_sources = lax.dynamic_slice_in_dim(sources, device_id * per_owner, per_owner)
    same_source = own_sources[:, None] == own_sources[None, :]
    sample_ids = jnp.arange(per_owner, dtype=jnp.int32)
    earlier = sample_ids[None, :] < sample_ids[:, None]
    rank_recv = jnp.sum(jnp.logical_and(same_source, earlier).astype(jnp.int32), axis=1)
    picked = jnp.take(incoming, own_sources * CAP + rank_recv, axis=1)
    sketch = picked * (1.0 / math.sqrt(total_samples))
    local_factor = householder_r(sketch.T)
    stacked = lax.all_gather(local_factor, ("rows", "sk"), axis=0, tiled=True)
    r_factor = householder_r(stacked)
    whitened = forward_solve(r_factor, picked)
    return (mixed, r_factor, whitened)


def solution(mesh):
    return jax.shard_map(
        local,
        mesh=mesh,
        in_specs=(P(None, ("rows", "sk")), P(("rows", "sk")), P(), P()),
        out_specs=(P(None, ("rows", "sk")), P(), P(None, ("rows", "sk"))),
        check_vma=False,
    )
```

profile of v0, /device:TPU:1, one launch (start us, length us, event | category | flops | bytes accessed | tf_op | source)
XLA Modules:
  0.0 1131.3 jit_solution(16419957727392758297)
XLA Ops:
  18.1 3.5 reshape.253
  21.6 11.5 %all-to-all-start = ((f32[128,1,2048]{2,1,0:T(1,128)}), f32[128,1,2048]{2,1,0:T(1,128)S(1)}, u32[]{:S(2)}, u32[]{:S(2)}) async-start(f32[128,1,2048]{2,1,0:T(1,128)} %reshape.253), calls=%async_computation | async-start | bytes 2097152 | tf_op jit(solution)/shard_map/all_to_all | solution.py:14
  37.2 3.5 reshape.249
  40.7 11.7 %all-to-all-done = f32[128,1,2048]{2,1,0:T(1,128)S(1)} async-done(((f32[128,1,2048]{2,1,0:T(1,128)}), f32[128,1,2048]{2,1,0:T(1,128)S(1)}, u32[]{:S(2)}, u32[]{:S(2)}) %all-to-all-start) | async-done | bytes 1048608 | tf_op jit(solution)/shard_map/all_to_all | solution.py:14
  52.4 5.2 all-to-all-start.2
  58.6 4.4 reduce.2
  67.1 3.1 copy.51
  72.5 4.1 all-to-all-done.2
  76.5 6.3 all-to-all-start.1
  82.9 60.7 %scatter_custom_fusion = s32[512]{0:T(512)S(1)} fusion(s32[16384]{0:T(1024)S(1)} %bitcast.167, s32[16384]{0:T(1024)} %param.13, s32[]{:T(128)} %constant.301.clone.1), kind=kCustom, calls=%fused_computation.101 | custom fusion | bytes 2560 | tf_op jit(solution)/shard_map/scatter | solution.py:103
  143.7 4.4 reduce
  157.5 10.2 all-to-all-start.3
  167.9 60.7 %scatter_custom_fusion.1 = f32[512]{0:T(512)S(1)} fusion(s32[16384]{0:T(1024)S(1)} %bitcast.168, f32[16384]{0:T(1024)S(1)} %broadcast.273, f32[]{:T(128)} %constant.312.clone.1), kind=kCustom, calls=%fused_computation.99 | custom fusion | bytes 2052 | tf_op jit(solution)/shard_map/scatter | solution.py:105
  229.0 4.4 reduce.3
  237.0 4.4 reduce.1
  244.9 6.5 maximum_multiply_fusion
  251.5 3.2 gather_fusion
  255.9 9.8 all-to-all-start.4
  266.0 9.6 all-to-all-done.4
  277.5 262.5 %while.47 = (s32[]{:T(128)}, f32[128,64]{0,1:T(8,128)S(1)}, s32[]{:T(128)}, f32[]{:T(128)}, f32[1]{0:T(128)}, /*index=5*/f32[1]{0:T(128)}, f32[1]{0:T(128)}) while((s32[]{:T(128)}, f32[128,64]{0,1:T(8,128)S(1)}, s32[]{:T(128)}, f32[]{:T(128)}, f32[1]{0:T(128)}, /*index=5*/f32[1]{0:T(128)}, f32[1]{0:T(128)}) %tuple.129), condition=%wide.region_7.8_spmd.clone.clone, body=%wide.region_4.7_spmd.clone.clone.sunk | while | flops 125060 | bytes 104623 | solution.py:52
  541.7 3.8 copy.67
  545.6 59.1 %all-gather.2.cloned.1.call-done = f32[8192,64]{1,0:T(8,128)} async-done(((f32[64,64]{1,0:T(8,128)}), f32[8192,64]{1,0:T(8,128)}) %all-gather.2.cloned.1.call-update) | async-done | bytes 2097168 | tf_op jit(solution)/shard_map/all_gather | solution.py:116
  607.5 418.9 %while.48 = (s32[]{:T(128)}, f32[8192,64]{0,1:T(8,128)S(1)}, s32[]{:T(128)}, f32[]{:T(128)}, f32[1]{0:T(128)}, /*index=5*/f32[1]{0:T(128)}, f32[1]{0:T(128)}) while((s32[]{:T(128)}, f32[8192,64]{0,1:T(8,128)S(1)}, s32[]{:T(128)}, f32[]{:T(128)}, f32[1]{0:T(128)}, /*index=5*/f32[1]{0:T(128)}, f32[1]{0:T(128)}) %tuple.132), condition=%wide.region_11.12_spmd.clone.clone, body=%wide.region_8.11_spmd.clone.clone.sunk | while | flops 7962628 | bytes 6701747 | solution.py:52
  1033.1 90.5 %while.46 = (s32[]{:T(128)}, f32[64,128]{1,0:T(8,128)S(1)}, f32[64,128]{1,0:T(8,128)S(1)}, f32[64,64]{1,0:T(8,128)S(1)}, s32[]{:T(128)}, /*index=5*/s32[]{:T(128)}, s32[]{:T(128)}) while((s32[]{:T(128)}, f32[64,128]{1,0:T(8,128)S(1)}, f32[64,128]{1,0:T(8,128)S(1)}, f32[64,64]{1,0:T(8,128)S(1)}, s32[]{:T(128)}, /*index=5*/s32[]{:T(128)}, ...), condition=%wide.region_13.14_spmd, body=%wide.region_12.13_spmd.sunk | while | flops 98563 | bytes 36973 | solution.py:70
  (1163 shorter events, 557.8 us)
Async XLA Ops:
  21.6 30.8 %all-to-all-start = ((f32[128,1,2048]{2,1,0:T(1,128)}), f32[128,1,2048]{2,1,0:T(1,128)S(1)}, u32[]{:S(2)}, u32[]{:S(2)}) async-start(f32[128,1,2048]{2,1,0:T(1,128)} %reshape.253), calls=%async_computation | async-start | bytes 2097152 | tf_op jit(solution)/shard_map/all_to_all | solution.py:14
  37.2 20.4 %copy-start.2 = (s32[16384,1]{0,1:T(1,128)S(1)}, s32[16384,1]{0,1:T(1,128)}, u32[]{:S(2)}) copy-start(s32[16384,1]{0,1:T(1,128)} %param.12) | copy-start | bytes 196612
  52.4 5.7 copy-start
  52.4 24.2 %all-to-all-start.2 = ((f32[128,1,2048]{2,1,0:T(1,128)}), f32[128,1,2048]{2,1,0:T(1,128)}, u32[]{:S(2)}, u32[]{:S(2)}) async-start(f32[128,1,2048]{2,1,0:T(1,128)} %reshape.249), calls=%async_computation.2 | async-start | bytes 2097152 | tf_op jit(solution)/shard_map/all_to_all | solution.py:14
  76.5 81.0 %all-to-all-start.1 = ((f32[128,1,2048]{2,1,0:T(1,128)}), f32[128,1,2048]{2,1,0:T(1,128)}, u32[]{:S(2)}, u32[]{:S(2)}) async-start(f32[128,1,2048]{2,1,0:T(1,128)} %reshape.255), calls=%async_computation.1 | async-start | bytes 2097152 | tf_op jit(solution)/shard_map/all_to_all | solution.py:91
  157.5 79.4 %all-to-all-start.3 = ((f32[128,1,2048]{2,1,0:T(1,128)}), f32[128,1,2048]{2,1,0:T(1,128)}, u32[]{:S(2)}, u32[]{:S(2)}) async-start(f32[128,1,2048]{2,1,0:T(1,128)} %reshape.251), calls=%async_computation.3 | async-start | bytes 2097152 | tf_op jit(solution)/shard_map/all_to_all | solution.py:91
  255.9 19.6 %all-to-all-start.4 = ((f32[128,1,256]{2,1,0:T(1,128)}), f32[128,1,256]{2,1,0:T(1,128)S(1)}, u32[]{:S(2)}, u32[]{:S(2)}) async-start(f32[128,1,256]{2,1,0:T(1,128)} %reshape.257), calls=%async_computation.4 | async-start | bytes 262144 | tf_op jit(solution)/shard_map/all_to_all | solution.py:107
  265.7 338.9 %all-gather.2.cloned.1.call-start = ((), (), s32[]{:S(2)}) async-start(), calls=%async_computation.5 | async-start | bytes 4227072 | tf_op jit(solution)/shard_map/all_gather | solution.py:116
  1123.7 0.6 copy-start.1
Sparse Core Ops, SparseCore 0:
  541.8 62.7 all-gather.1
where the time goes:
time: 1140 us; the launch traced here: 1130 us
  local copies, waits for them, and re-layouts  298 us (26%)
  loops' own time  269 us (24%)
  other arithmetic  245 us (21%)
  matrix products  177 us (16%)
  waiting for transfers between devices  84.4 us (7%)
  starting transfers between devices  43.2 us (4%)
  between operations  14.6 us (1%)
    another operation x2, loops' own time, householder_r(): reduced = lax.fori_loop(0, cols_count, reflect, matrix)  268 us
    dot_general x128, matrix products, reflect(): projection = jnp.dot(vector, current, precision=lax.Precision.HIGHEST)  119 us
    reduce_sum x128, other arithmetic, reflect(): denominator = jnp.sum(vector * vector)  79.7 us
    dynamic_slice x128, local copies, waits for them, and re-layouts, reflect(): pivot_value = column[j]  79.7 us
    reduce_sum x128, other arithmetic, reflect(): length = jnp.sqrt(jnp.sum(column * column))  77.9 us
    scatter x1, local copies, waits for them, and re-layouts, local(): jnp.zeros((device_count * CAP,), jnp.int32).at[slot_number]  60.7 us
    scatter x1, local copies, waits for them, and re-layouts, local(): jnp.zeros((device_count * CAP,), jnp.float32).at[slot_number]  60.7 us
    all_gather x1, waiting for transfers between devices, local(): stacked = lax.all_gather(local_factor, ('rows', 'sk'), axis=0, tiled=True)  59.1 us
  transfers between devices with their start and end apart: 6, of which 4 were waited for; matrix products, arithmetic and copies ran while one was open for 15% of the time, Pallas kernels for 0%

commit v1 on v0

v1 whole, which is shorter than its diff:
```python
import math

import jax
import jax.numpy as jnp
from jax import lax
from jax.experimental import pallas as pl
from jax.experimental.pallas import tpu as pltpu
from jax.sharding import PartitionSpec as P

F32, BF16, I32 = jnp.float32, jnp.bfloat16, jnp.int32
AXES = ("rows", "sk")
DEVS, COLS, HALF, LANES, CAP = 128, 64, 32, 128, 4


def split3(x):
    top = x.astype(BF16)
    rest = x - top.astype(F32)
    mid = rest.astype(BF16)
    low = (rest - mid.astype(F32)).astype(BF16)
    return top, mid, low


def dot_nn(a, b):
    return lax.dot_general(a, b, (((1,), (0,)), ((), ())), preferred_element_type=F32)


def dot_nt(a, b):
    return lax.dot_general(a, b, (((1,), (1,)), ((), ())), preferred_element_type=F32)


def dot_tn(a, b):
    return lax.dot_general(a, b, (((0,), (0,)), ((), ())), preferred_element_type=F32)


def iota(shape, dim):
    return lax.broadcasted_iota(I32, shape, dim)


def butterflies(values):
    size, step = len(values), 1
    while step < size:
        nxt = list(values)
        for i in range(size):
            if not i & step:
                nxt[i] = values[i] + values[i + step]
                nxt[i + step] = values[i] - values[i + step]
        values, step = nxt, step * 2
    return values


def lane_table():
    k, n = iota((256, 256), 0), iota((256, 256), 1)
    bits = jnp.bitwise_and(k % 128, (n // 128) * 64 + n % 64)
    for shift in (4, 2, 1):
        bits = jnp.bitwise_xor(bits, lax.shift_right_logical(bits, shift))
    sign = 1.0 - 2.0 * jnp.bitwise_and(bits, 1).astype(F32)
    return jnp.where(k // 128 == (n % 128) // 64, sign, 0.0).astype(BF16)


def local_mix(panel, signs, table, send):
    table[...] = lane_table()

    def first(high, carry):
        at = pl.ds(pl.multiple_of(high * 1024, 1024), 1024)
        x = panel[:, at] * signs[:, at].astype(F32)
        lhs = jnp.concatenate(
            [
                jnp.concatenate([x[:HALF, 128 * b : 128 * b + 128], x[HALF:, 128 * b : 128 * b + 128]], axis=1)
                for b in range(8)
            ],
            axis=0,
        )
        weights = table[...]
        top, mid, low = split3(lhs)
        out = dot_nn(low, weights) + dot_nn(mid, weights) + dot_nn(top, weights)
        done = butterflies([out[32 * b : 32 * b + 32] for b in range(8)])
        for b in range(8):
            send[16 * high + 2 * b] = done[b][:, :128]
            send[16 * high + 2 * b + 1] = done[b][:, 128:]
        return carry

    lax.fori_loop(0, 8, first, 0)

    def second(low, carry):
        done = butterflies([send[16 * high + low] for high in range(8)])
        for high in range(8):
            send[16 * high + low] = done[high]
        return carry

    lax.fori_loop(0, 16, second, 0)


def combine(data):
    def first(i, carry):
        high, group = i // 4, i % 4
        at = pl.ds(pl.multiple_of(group * 8, 8), 8)
        done = butterflies([data[16 * high + low, at] for low in range(16)])
        for low in range(16):
            data[16 * high + low, at] = done[low]
        return carry

    lax.fori_loop(0, 32, first, 0)

    def second(low, carry):
        done = butterflies([data[16 * high + low] for high in range(8)])
        for high in range(8):
            data[16 * high + low] = done[high]
        return carry

    lax.fori_loop(0, 16, second, 0)


def unpack(a, b):
    left = iota((HALF, LANES), 1) < 64
    upper = jnp.where(left, a, pltpu.roll(b, 64, 1))
    lower = jnp.where(left, pltpu.roll(a, 64, 1), b)
    return jnp.concatenate([upper, lower], axis=0)


def count_rows(sources, offsets, counts, me):
    counts[...] = jnp.zeros_like(counts)

    def step(i, carry):
        at = pl.ds(pl.multiple_of(i * 8, 8), 8)
        src8, rel8 = sources[at, :], offsets[at, :] - me * 64
        inside = jnp.logical_and(rel8 >= 0, rel8 < 64)
        lane8 = jnp.where(inside, rel8 + jnp.where(src8 >= 64, 64, 0), -1)
        q8 = jnp.bitwise_and(src8, 63)
        total = counts[...]
        for pair in range(4):
            q = jnp.concatenate([q8[2 * pair : 2 * pair + 1], q8[2 * pair + 1 : 2 * pair + 2]], axis=1)
            lane = jnp.concatenate([lane8[2 * pair : 2 * pair + 1], lane8[2 * pair + 1 : 2 * pair + 2]], axis=1)
            left = jnp.where(iota((64, 256), 0) == q, 1.0, 0.0).astype(BF16)
            right = jnp.where(iota((128, 256), 0) == lane, 1.0, 0.0).astype(BF16)
            total = total + dot_nt(left, right)
        counts[...] = total
        return carry

    lax.fori_loop(0, 16, step, 0)


def gram(data, counts, acc):
    acc[...] = jnp.zeros_like(acc)

    def step(i, carry):
        x = jnp.concatenate([unpack(data[2 * i], data[2 * i + 64]), unpack(data[2 * i + 1], data[2 * i + 65])], axis=1)
        w = jnp.concatenate([counts[pl.ds(2 * i, 1), :], counts[pl.ds(2 * i + 1, 1), :]], axis=1)
        plain = jnp.concatenate(split3(x), axis=0)
        weighted = jnp.concatenate(split3(x * w), axis=0)
        acc[...] += dot_nt(weighted, plain)
        return carry

    lax.fori_loop(0, 32, step, 0)
    block = lambda i, j: acc[64 * i : 64 * i + 64, 64 * j : 64 * j + 64]
    small = block(2, 2) + (block(1, 2) + block(2, 1))
    small = small + (block(0, 2) + block(2, 0)) + block(1, 1)
    return small + (block(0, 1) + block(1, 0)) + block(0, 0)


def factor(g):
    sub, lane = iota((COLS, LANES), 0), iota((COLS, LANES), 1)
    m = jnp.concatenate([g, jnp.where(sub == lane, 1.0, 0.0)[:, :64]], axis=1)
    subs = iota((COLS, 1), 0)
    for j in range(COLS):
        pivot_row = m[j : j + 1, :]
        inverse = 1.0 / m[j : j + 1, j : j + 1]
        lead = jnp.where(subs > j, m[:, j : j + 1] * inverse, 0.0)
        m = m - lead * pivot_row
    diagonal = jnp.sum(jnp.where(sub == lane, m, 0.0), axis=1, keepdims=True)
    scaled = m / jnp.sqrt(diagonal)
    return jnp.where(jnp.logical_or(lane >= sub, lane >= 64), scaled, 0.0)


def earlier():
    return jnp.where(iota((128, 128), 0) < iota((128, 128), 1), 1.0, 0.0).astype(BF16)


def slot_places(sources, offsets, me):
    mine = sources[...] == me
    rank = dot_nn(jnp.where(mine, 1.0, 0.0).astype(BF16), earlier())
    high = (offsets[...] // 128).astype(F32)
    low = (offsets[...] % 128).astype(F32)
    ones = jnp.ones((8, 128), BF16)
    places = []
    for r in range(CAP):
        chosen = jnp.logical_and(mine, rank == float(r))
        places.append(
            tuple(dot_nt(ones, jnp.where(chosen, v, 0.0).astype(BF16)).astype(I32) for v in (high, low))
        )
    return places


def finish(back, places, mixed, scale):
    highs = [jnp.concatenate([high] * 8, axis=0) for high, _ in places]
    lows = [jnp.concatenate([low] * 8, axis=0) for _, low in places]

    def step(b, picked):
        x = unpack(back[2 * b], back[2 * b + 1]) * scale
        mixed[:, pl.ds(pl.multiple_of(b * 128, 128), 128)] = x
        return tuple(
            jnp.where(high == b, jnp.take_along_axis(x, low, axis=1, mode="promise_in_bounds"), old)
            for high, low, old in zip(highs, lows, picked)
        )

    return lax.fori_loop(0, 64, step, tuple(jnp.zeros((COLS, LANES), F32) for _ in range(CAP)))


def exact6(a, b, dot):
    a1, a2, a3 = split3(a)
    b1, b2, b3 = split3(b)
    small = dot(a2, b2) + (dot(a1, b3) + dot(a3, b1))
    return small + (dot(a1, b2) + dot(a2, b1)) + dot(a1, b1)


def whiten_slots(picked, inverse, out):
    done = [exact6(p.T, inverse, dot_nt) for p in picked]
    for pair in range(2):
        out[:, pair, :] = jnp.concatenate(done[2 * pair : 2 * pair + 2], axis=1)


def place_samples(incoming, own):
    hot = iota((128, 128), 0) == own
    flag = jnp.where(hot, 1.0, 0.0)
    rank = dot_nn(flag.astype(BF16), earlier())
    total = jnp.zeros((COLS, LANES), F32)
    for pair in range(2):
        top, mid, low = split3(incoming[:, pair, :])
        for half in range(2):
            chosen = jnp.where(rank == float(2 * pair + half), flag, 0.0).astype(BF16)
            got = dot_tn(low, chosen) + dot_tn(mid, chosen) + dot_tn(top, chosen)
            total = total + got[64 * half : 64 * half + 64]
    return total


def my_id():
    return lax.axis_index("rows") * 4 + lax.axis_index("sk")


def call(body, out, *args, scratch=(), smem=()):
    spec = pl.BlockSpec(memory_space=pltpu.VMEM)
    return pl.pallas_call(
        body,
        out_shape=out,
        in_specs=[pl.BlockSpec(memory_space=pltpu.SMEM) if i in smem else spec for i in range(len(args))],
        out_specs=jax.tree.map(lambda _: spec, out),
        scratch_shapes=list(scratch),
        compiler_params=pltpu.CompilerParams(vmem_limit_bytes=56 << 20),
    )(*args)


def shape(*dims):
    return jax.ShapeDtypeStruct(dims, F32)


def local(panel, signs, sample_device, sample_offset):
    me = my_id().astype(I32).reshape(1)
    sources = sample_device.reshape(128, 128)
    offsets = sample_offset.reshape(128, 128)

    def mix(panel_ref, signs_ref, send, table):
        local_mix(panel_ref, signs_ref, table, send)

    blocks = shape(DEVS, HALF, LANES)
    send = call(mix, blocks, panel, signs.reshape(1, -1), scratch=[pltpu.VMEM((256, 256), BF16)])
    arrived = lax.all_to_all(send, AXES, split_axis=0, concat_axis=0, tiled=True)

    def middle(me_ref, arrived_ref, src, off, data, g, counts, acc):
        data[...] = arrived_ref[...]
        combine(data)
        count_rows(src, off, counts, me_ref[0])
        g[...] = gram(data, counts, acc)

    data, g = call(
        middle, (blocks, shape(64, 64)), me, arrived, sources, offsets,
        scratch=[pltpu.VMEM((64, 128), F32), pltpu.VMEM((192, 192), F32)], smem=(0,),
    )
    back = lax.all_to_all(data, AXES, split_axis=0, concat_axis=0, tiled=True)
    total = lax.psum(g, AXES)

    def chol(g_ref, out):
        out[...] = factor(g_ref[...] * (2.0**-34))

    both = call(chol, shape(64, 128), total)

    def last(me_ref, back_ref, src, off, both_ref, mixed, slots):
        places = slot_places(src, off, me_ref[0])
        picked = finish(back_ref, places, mixed, 2.0**-10)
        whiten_slots(picked, both_ref[:, 64:], slots)

    mixed, slots = call(
        last, (shape(64, 8192), shape(DEVS, 2, LANES)), me, back, sources, offsets, both, smem=(0,)
    )
    incoming = lax.all_to_all(slots, AXES, split_axis=0, concat_axis=0, tiled=True)
    own = lax.dynamic_slice_in_dim(sources, me[0], 1, 0)

    def place(incoming_ref, own_ref, out):
        out[...] = place_samples(incoming_ref, own_ref[...])

    whitened = call(place, shape(64, 128), incoming, own)
    return mixed, both[:, :64], whitened


def solution(mesh):
    return jax.shard_map(
        local,
        mesh=mesh,
        in_specs=(P(None, AXES), P(AXES), P(), P()),
        out_specs=(P(None, AXES), P(), P(None, AXES)),
        check_vma=False,
    )
```

time: 1140 us -> 195 us (0.17)
  local copies, waits for them, and re-layouts: 298 us -> 4.48 us
  loops' own time: 269 us -> 0 us
  other arithmetic: 245 us -> 0 us
  matrix products: 177 us -> 0 us
  blocking collectives: 0 us -> 81.8 us
  Pallas kernels: 0 us -> 46.6 us
  waiting for transfers between devices: 84.4 us -> 39.2 us
  starting transfers between devices: 43.2 us -> 21.9 us
  between operations: 14.6 us -> 0.68 us
    another operation x3 -> x0, loops' own time: 269 us -> none  [the longest x2 268 us: householder_r(): reduced = lax.fori_loop(0, cols_count, reflect, matrix)]
    dot_general x194 -> x0, matrix products: 173 us -> none  [the longest x128 119 us: reflect(): projection = jnp.dot(vector, current, precision=lax.Precision.HIGHEST)]
    reduce_sum x257 -> x0, other arithmetic: 158 us -> none  [the longest x128 79.7 us: reflect(): denominator = jnp.sum(vector * vector)]
    scatter x2 -> x0, local copies, waits for them, and re-layouts: 121 us -> none  [the longest x1 60.7 us: local(): jnp.zeros((device_count * CAP,), jnp.int32).at[slot_number]]
    dynamic_slice x256 -> x1, local copies, waits for them, and re-layouts: 119 us -> 1.18 us  [local(): own = lax.dynamic_slice_in_dim(sources, me[0], 1, 0)]
    psum x0 -> x1, blocking collectives: none -> 81.8 us  [local(): total = lax.psum(g, AXES)]
    all_gather x1 -> x0, waiting for transfers between devices: 59.1 us -> none  [local(): stacked = lax.all_gather(local_factor, ('rows', 'sk'), axis=0, tiled=True)]
    sub x128 -> x0, other arithmetic: 49.5 us -> none  [reflect(): return current - vector[:, None] * projection[None, :] * (2.0 / denominator)]
  transfers between devices with their start and end apart: 6 -> 3, of which waited for: 4 -> 2; matrix products, arithmetic and copies ran while one was open for 15% -> 1% of each run, Pallas kernels for 0% -> 3%
where the time goes in v1:
time: 195 us
  blocking collectives  81.8 us (42%)
  Pallas kernels  46.6 us (24%)
  waiting for transfers between devices  39.2 us (20%)
  starting transfers between devices  21.9 us (11%)
  local copies, waits for them, and re-layouts  4.48 us (2%)
    psum x1, blocking collectives, local(): total = lax.psum(g, AXES)  81.8 us
    pallas_call x5, Pallas kernels, call(): pl.pallas_call(body, out_shape=out, in_specs=[pl.BlockSpec(memory_space=p...  46.6 us
    all_to_all x1, waiting for transfers between devices, local(): lax.all_to_all(send, AXES, split_axis=0, concat_axis=0, tiled=True)  30.5 us
    all_to_all x1, starting transfers between devices, local(): lax.all_to_all(send, AXES, split_axis=0, concat_axis=0, tiled=True)  11.5 us
    all_to_all x1, waiting for transfers between devices, local(): lax.all_to_all(slots, AXES, split_axis=0, concat_axis=0, tiled=True)  8.64 us
    all_to_all x1, starting transfers between devices, local(): lax.all_to_all(slots, AXES, split_axis=0, concat_axis=0, tiled=True)  6.59 us
  transfers between devices with their start and end apart: 3, of which 2 were waited for; matrix products, arithmetic and copies ran while one was open for 1% of the time, Pallas kernels for 3%

profile of v1, /device:TPU:1, one launch (start us, length us, event | category | flops | bytes accessed | tf_op | source)
XLA Modules:
  0.0 194.6 jit_solution(9207513072409418104)
XLA Ops:
  0.6 5.8 %shard_map.67 = f32[128,32,128]{2,1,0:T(8,128)} custom-call(f32[64,8192]{1,0:T(8,128)} %panel_ref.1, s32[1,8192]{1,0:T(1,128)} %bitcast.11), custom_call_target="tpu_custom_call" | custom-call | tf_op jit(solution)/shard_map/pallas_call | solution.py:241
  6.4 11.5 %all-to-all-start = ((f32[128,32,128]{2,1,0:T(8,128)}), f32[128,32,128]{2,1,0:T(8,128)S(1)}, u32[]{:S(2)}, u32[]{:S(2)}) async-start(f32[128,32,128]{2,1,0:T(8,128)} %shard_map.67), calls=%async_computation | async-start | bytes 4194304 | tf_op jit(solution)/shard_map/all_to_all | solution.py:265
  17.9 30.5 %all-to-all-done.arrived_ref = f32[128,32,128]{2,1,0:T(8,128)S(1)} async-done(((f32[128,32,128]{2,1,0:T(8,128)}), f32[128,32,128]{2,1,0:T(8,128)S(1)}, u32[]{:S(2)}, u32[]{:S(2)}) %all-to-all-start) | async-done | bytes 2097184 | tf_op jit(solution)/shard_map/all_to_all | solution.py:265
  48.4 0.0 copy-start
  48.4 1.3 copy-done
  49.7 16.5 %shard_map.68 = (f32[128,32,128]{2,1,0:T(8,128)}, f32[64,64]{1,0:T(8,128)}) custom-call(s32[1]{0:T(128)} %bitcast.me_ref, f32[128,32,128]{2,1,0:T(8,128)} %copy-done, s32[128,128]{1,0:T(8,128)} %bitcast.7, s32[128,128]{1,0:T(8,128)} %bitcast.5), custom_call_target="tpu_custom_call" | custom-call | tf_op jit(solution)/shard_map/pallas_call | solution.py:241
  66.3 0.0 copy-start.3
  66.3 3.8 %all-to-all-start.1 = ((f32[128,32,128]{2,1,0:T(8,128)}), f32[128,32,128]{2,1,0:T(8,128)S(1)}, u32[]{:S(2)}, u32[]{:S(2)}) async-start(f32[128,32,128]{2,1,0:T(8,128)} %get-tuple-element.7), calls=%async_computation.1 | async-start | bytes 4194304 | tf_op jit(solution)/shard_map/all_to_all | solution.py:277
  70.1 0.0 copy-done.3
  70.1 81.8 %psum.7.g_ref = f32[64,64]{1,0:T(8,128)} all-reduce(f32[64,64]{1,0:T(8,128)S(1)} %copy-done.3), channel_id=1, replica_groups=mesh['rows'=32,'sk'=4] {'rows','sk'}, use_global_device_ids=true, to_apply=%region_0.0 | all-reduce | flops 4096 | bytes 32768 | tf_op jit(solution)/shard_map/psum | solution.py:278
  151.9 6.8 %shard_map.69.both_ref = f32[64,128]{1,0:T(8,128)} custom-call(f32[64,64]{1,0:T(8,128)} %psum.7.g_ref), custom_call_target="tpu_custom_call" | custom-call | tf_op jit(solution)/shard_map/pallas_call | solution.py:241
  158.7 0.0 all-to-all-done.1.back_ref
  158.7 0.0 copy-start.1
  158.7 1.3 copy-done.1
  160.1 15.2 %shard_map.70 = (f32[64,8192]{1,0:T(8,128)}, f32[128,2,128]{2,1,0:T(2,128)}) custom-call(s32[1]{0:T(128)} %bitcast.me_ref, f32[128,32,128]{2,1,0:T(8,128)} %copy-done.1, s32[128,128]{1,0:T(8,128)} %bitcast.8, s32[128,128]{1,0:T(8,128)} %bitcast.6, f32[64,128]{1,0:T(8,128)} %shard_map.69.both_ref), custom_call_target="tpu_custom_call" | custom-call | tf_op jit(solution)/shard_map/pallas_call | solution.py:241
  175.2 6.6 %all-to-all-start.2 = ((f32[128,2,128]{2,1,0:T(2,128)}), f32[128,2,128]{2,1,0:T(2,128)S(1)}, u32[]{:S(2)}, u32[]{:S(2)}) async-start(f32[128,2,128]{2,1,0:T(2,128)} %get-tuple-element.10), calls=%async_computation.2 | async-start | bytes 262144 | tf_op jit(solution)/shard_map/all_to_all | solution.py:293
  181.8 1.2 constant_dynamic-slice_fusion.own_ref
  183.0 8.6 %all-to-all-done.2.incoming_ref = f32[128,2,128]{2,1,0:T(2,128)S(1)} async-done(((f32[128,2,128]{2,1,0:T(2,128)}), f32[128,2,128]{2,1,0:T(2,128)S(1)}, u32[]{:S(2)}, u32[]{:S(2)}) %all-to-all-start.2) | async-done | bytes 131104 | tf_op jit(solution)/shard_map/all_to_all | solution.py:293
  191.6 0.0 copy-start.2
  191.6 0.6 copy-done.2
  192.3 2.3 %shard_map.71 = f32[64,128]{1,0:T(8,128)} custom-call(f32[128,2,128]{2,1,0:T(2,128)} %copy-done.2, s32[1,128]{1,0:T(1,128)} %constant_dynamic-slice_fusion.own_ref), custom_call_target="tpu_custom_call" | custom-call | tf_op jit(solution)/shard_map/pallas_call | solution.py:241
Async XLA Ops:
  6.4 42.0 %all-to-all-start = ((f32[128,32,128]{2,1,0:T(8,128)}), f32[128,32,128]{2,1,0:T(8,128)S(1)}, u32[]{:S(2)}, u32[]{:S(2)}) async-start(f32[128,32,128]{2,1,0:T(8,128)} %shard_map.67), calls=%async_computation | async-start | bytes 4194304 | tf_op jit(solution)/shard_map/all_to_all | solution.py:265
  48.4 1.3 copy-start
  66.3 3.8 %copy-start.3 = (f32[64,64]{1,0:T(8,128)S(1)}, f32[64,64]{1,0:T(8,128)}, u32[]{:S(2)}) copy-start(f32[64,64]{1,0:T(8,128)} %get-tuple-element.8) | copy-start | bytes 49156
  66.3 92.5 %all-to-all-start.1 = ((f32[128,32,128]{2,1,0:T(8,128)}), f32[128,32,128]{2,1,0:T(8,128)S(1)}, u32[]{:S(2)}, u32[]{:S(2)}) async-start(f32[128,32,128]{2,1,0:T(8,128)} %get-tuple-element.7), calls=%async_computation.1 | async-start | bytes 4194304 | tf_op jit(solution)/shard_map/all_to_all | solution.py:277
  158.7 1.3 copy-start.1
  175.2 16.4 %all-to-all-start.2 = ((f32[128,2,128]{2,1,0:T(2,128)}), f32[128,2,128]{2,1,0:T(2,128)S(1)}, u32[]{:S(2)}, u32[]{:S(2)}) async-start(f32[128,2,128]{2,1,0:T(2,128)} %get-tuple-element.10), calls=%async_computation.2 | async-start | bytes 262144 | tf_op jit(solution)/shard_map/all_to_all | solution.py:293
  191.6 0.6 copy-start.2

commit v2 on v1

--- a/solution.py
+++ b/solution.py
@@ -1,5 +1,3 @@
-import math
-
 import jax
 import jax.numpy as jnp
 from jax import lax
@@ -55,17 +53,25 @@
         bits = jnp.bitwise_xor(bits, lax.shift_right_logical(bits, shift))
     sign = 1.0 - 2.0 * jnp.bitwise_and(bits, 1).astype(F32)
     return jnp.where(k // 128 == (n % 128) // 64, sign, 0.0).astype(BF16)
-
-
-def local_mix(panel, signs, table, send):
-    table[...] = lane_table()
+SPLIT = 72
+
+
+PARTS = 2
+ROWS = HALF // PARTS
+MESH = pl.DeviceIdType.MESH
+
+
+def local_mix(part, panel, signs, table, send):
+    at_rows = pl.ds(part * ROWS, ROWS)
 
     def first(high, carry):
         at = pl.ds(pl.multiple_of(high * 1024, 1024), 1024)
-        x = panel[:, at] * signs[:, at].astype(F32)
+        sign = signs[:, at].astype(F32)
+        upper = panel[part * ROWS : part * ROWS + ROWS, at] * sign
+        lower = panel[HALF + part * ROWS : HALF + part * ROWS + ROWS, at] * sign
         lhs = jnp.concatenate(
             [
-                jnp.concatenate([x[:HALF, 128 * b : 128 * b + 128], x[HALF:, 128 * b : 128 * b + 128]], axis=1)
+                jnp.concatenate([upper[:, 128 * b : 128 * b + 128], lower[:, 128 * b : 128 * b + 128]], axis=1)
                 for b in range(8)
             ],
             axis=0,
@@ -73,38 +79,39 @@
         weights = table[...]
         top, mid, low = split3(lhs)
         out = dot_nn(low, weights) + dot_nn(mid, weights) + dot_nn(top, weights)
-        done = butterflies([out[32 * b : 32 * b + 32] for b in range(8)])
+        done = butterflies([out[ROWS * b : ROWS * b + ROWS] for b in range(8)])
         for b in range(8):
-            send[16 * high + 2 * b] = done[b][:, :128]
-            send[16 * high + 2 * b + 1] = done[b][:, 128:]
+            send[16 * high + 2 * b, at_rows] = done[b][:, :128]
+            send[16 * high + 2 * b + 1, at_rows] = done[b][:, 128:]
         return carry
 
     lax.fori_loop(0, 8, first, 0)
 
     def second(low, carry):
-        done = butterflies([send[16 * high + low] for high in range(8)])
+        done = butterflies([send[16 * high + low, at_rows] for high in range(8)])
         for high in range(8):
-            send[16 * high + low] = done[high]
+            send[16 * high + low, at_rows] = done[high]
         return carry
 
     lax.fori_loop(0, 16, second, 0)
 
 
-def combine(data):
+def combine(part, data):
     def first(i, carry):
-        high, group = i // 4, i % 4
-        at = pl.ds(pl.multiple_of(group * 8, 8), 8)
+        high, group = i // (ROWS // 8), i % (ROWS // 8)
+        at = pl.ds(pl.multiple_of(part * ROWS + group * 8, 8), 8)
         done = butterflies([data[16 * high + low, at] for low in range(16)])
         for low in range(16):
             data[16 * high + low, at] = done[low]
         return carry
 
-    lax.fori_loop(0, 32, first, 0)
+    lax.fori_loop(0, 8 * (ROWS // 8), first, 0)
+    at_rows = pl.ds(part * ROWS, ROWS)
 
     def second(low, carry):
-        done = butterflies([data[16 * high + low] for high in range(8)])
+        done = butterflies([data[16 * high + low, at_rows] for high in range(8)])
         for high in range(8):
-            data[16 * high + low] = done[high]
+            data[16 * high + low, at_rows] = done[high]
         return carry
 
     lax.fori_loop(0, 16, second, 0)
@@ -190,19 +197,41 @@
     return places
 
 
-def finish(back, places, mixed, scale):
-    highs = [jnp.concatenate([high] * 8, axis=0) for high, _ in places]
-    lows = [jnp.concatenate([low] * 8, axis=0) for _, low in places]
-
-    def step(b, picked):
-        x = unpack(back[2 * b], back[2 * b + 1]) * scale
-        mixed[:, pl.ds(pl.multiple_of(b * 128, 128), 128)] = x
-        return tuple(
-            jnp.where(high == b, jnp.take_along_axis(x, low, axis=1, mode="promise_in_bounds"), old)
-            for high, low, old in zip(highs, lows, picked)
-        )
-
-    return lax.fori_loop(0, 64, step, tuple(jnp.zeros((COLS, LANES), F32) for _ in range(CAP)))
+def unpack_part(part, back, mixed, scale):
+    def step(b, carry):
+        at = pl.ds(pl.multiple_of(b * 128, 128), 128)
+        one, two = back[2 * b, pl.ds(part * ROWS, ROWS)], back[2 * b + 1, pl.ds(part * ROWS, ROWS)]
+        left = iota((ROWS, LANES), 1) < 64
+        mixed[part * ROWS : part * ROWS + ROWS, at] = jnp.where(left, one, pltpu.roll(two, 64, 1)) * scale
+        mixed[HALF + part * ROWS : HALF + part * ROWS + ROWS, at] = jnp.where(left, pltpu.roll(one, 64, 1), two) * scale
+        return carry
+
+    lax.fori_loop(0, 64, step, 0)
+
+
+def pick_part(part, mixed, places, picked):
+    for r, (high, low) in enumerate(places):
+        high = jnp.concatenate([high] * (ROWS // 8), axis=0)
+        low = jnp.concatenate([low] * (ROWS // 8), axis=0)
+
+        def step(i, found):
+            for k in range(4):
+                b = 4 * i + k
+                at = pl.ds(pl.multiple_of(b * 128, 128), 128)
+                found = tuple(
+                    jnp.where(
+                        high == b,
+                        jnp.take_along_axis(mixed[base : base + ROWS, at], low, axis=1, mode="promise_in_bounds"),
+                        old,
+                    )
+                    for base, old in zip((part * ROWS, HALF + part * ROWS), found)
+                )
+            return found
+
+        zero = jnp.zeros((ROWS, LANES), F32)
+        upper, lower = lax.fori_loop(0, 16, step, (zero, zero))
+        picked[r, part * ROWS : part * ROWS + ROWS] = upper
+        picked[r, HALF + part * ROWS : HALF + part * ROWS + ROWS] = lower
 
 
 def exact6(a, b, dot):
@@ -232,72 +261,175 @@
     return total
 
 
-def my_id():
-    return lax.axis_index("rows") * 4 + lax.axis_index("sk")
-
-
-def call(body, out, *args, scratch=(), smem=()):
-    spec = pl.BlockSpec(memory_space=pltpu.VMEM)
+def position():
+    row, y = lax.axis_index("rows"), lax.axis_index("sk")
+    return row // 8, (row // 2) % 4, row % 2, y
+
+
+def device(z, x, c, y):
+    return ((z * 4 + x) * 2 + c, y)
+
+
+def flat(z, x, c, y):
+    return ((z * 4 + x) * 2 + c) * 4 + y
+
+
+def peer(t):
+    z, x, c, y = position()
+    u = t // 2
+    a, b, e = u % 4, (u // 4) % 4, u // 16
+    return (z + a + 2 * b + e) % 4, (x + a + b) % 4, (c + t) % 2, (y + a) % 4
+
+
+def start(src, dst, send_sem, recv_sem, where):
+    pltpu.make_async_remote_copy(
+        src_ref=src, dst_ref=dst, send_sem=send_sem, recv_sem=recv_sem, device_id=device(*where), device_id_type=MESH
+    ).start()
+
+
+def settle(ref, send_sem, recv_sem):
+    whole = pltpu.make_async_remote_copy(
+        src_ref=ref, dst_ref=ref, send_sem=send_sem, recv_sem=recv_sem, device_id=device(*peer(1)), device_id_type=MESH
+    )
+    whole.wait_recv()
+    whole.wait_send()
+
+
+def kernel(
+    panel_hbm, signs, sources, offsets, mixed, factor_out, whitened,
+    panel, table, send, arrived, back, counts, acc, first_sums, second_sums, picked, slots, incoming,
+    out_send, out_recv, back_send, back_recv, one_send, one_recv, two_send, two_recv, slot_send, slot_recv, load_sem,
+):
+    z, x, c, y = position()
+    me = flat(z, x, c, y)
+    barrier = pltpu.get_barrier_semaphore()
+    loads = [
+        pltpu.make_async_copy(panel_hbm.at[pl.ds(8 * g, 8)], panel.at[pl.ds(8 * g, 8)], load_sem.at[g]) for g in range(8)
+    ]
+    for load in loads:
+        load.start()
+
+    def greet(t, carry):
+        pl.semaphore_signal(barrier, inc=1, device_id=device(*peer(t)), device_id_type=MESH)
+        return carry
+
+    lax.fori_loop(1, 128, greet, 0)
+    table[...] = lane_table()
+    rows = lambda part: pl.ds(part * ROWS, ROWS)
+
+    def send_out(part):
+        def step(t, carry):
+            where = peer(t)
+            start(send.at[flat(*where), rows(part)], arrived.at[me, rows(part)], out_send.at[part], out_recv.at[part], where)
+            return carry
+
+        lax.fori_loop(1, 128, step, 0)
+        arrived[me, rows(part)] = send[me, rows(part)]
+
+    def send_back(part, low, high):
+        def step(t, carry):
+            where = peer(t)
+            start(arrived.at[flat(*where), rows(part)], back.at[me, rows(part)], back_send.at[part], back_recv.at[part], where)
+            return carry
+
+        lax.fori_loop(low, high, step, 0)
+
+    for part in range(PARTS):
+        for g in range(8):
+            if (g % 4) * 8 // ROWS == part:
+                loads[g].wait()
+        local_mix(part, panel, signs, table, send)
+        if part == 0:
+            pl.semaphore_wait(barrier, 127)
+        send_out(part)
+    count_rows(sources, offsets, counts, me)
+    places = slot_places(sources, offsets, me)
+    for part in range(PARTS):
+        settle(arrived.at[pl.ds(0, 127), rows(part)], out_send.at[part], out_recv.at[part])
+        combine(part, arrived)
+        send_back(part, 1, 128 if part < PARTS - 1 else SPLIT)
+        back[me, rows(part)] = arrived[me, rows(part)]
+
+    g = gram(arrived, counts, acc)
+    mine = c * 4 + y
+    first_sums[mine] = jnp.concatenate([g[:32], g[32:]], axis=1)
+
+    def step_one(t, carry):
+        where = (z, x, (c + t) % 2, (y + t // 2) % 4)
+        start(first_sums.at[mine], first_sums.at[mine], one_send, one_recv, where)
+        return carry
+
+    lax.fori_loop(1, 8, step_one, 0)
+    send_back(PARTS - 1, SPLIT, 128)
+    settle(first_sums.at[pl.ds(0, 7)], one_send, one_recv)
+    total = first_sums[0]
+    for i in range(1, 8):
+        total = total + first_sums[i]
+    line = z * 4 + x
+    second_sums[line] = total
+
+    def step_two(t, carry):
+        where = ((z + t // 4) % 4, (x + t) % 4, c, y)
+        start(second_sums.at[line], second_sums.at[line], two_send, two_recv, where)
+        return carry
+
+    lax.fori_loop(1, 16, step_two, 0)
+    for part in range(PARTS - 1):
+        settle(back.at[pl.ds(0, 127), rows(part)], back_send.at[part], back_recv.at[part])
+        unpack_part(part, back, mixed, 2.0**-10)
+        pick_part(part, mixed, places, picked)
+    settle(second_sums.at[pl.ds(0, 15)], two_send, two_recv)
+    total = second_sums[0]
+    for i in range(1, 16):
+        total = total + second_sums[i]
+    both = factor(jnp.concatenate([total[:, :64], total[:, 64:]], axis=0) * (2.0**-34))
+    factor_out[...] = both[:, :64]
+
+    last = PARTS - 1
+    settle(back.at[pl.ds(0, 127), rows(last)], back_send.at[last], back_recv.at[last])
+    unpack_part(last, back, mixed, 2.0**-10)
+    pick_part(last, mixed, places, picked)
+    whiten_slots([picked[r] for r in range(CAP)], both[:, 64:], slots)
+
+    def step_slots(t, carry):
+        where = peer(t)
+        start(slots.at[flat(*where)], incoming.at[me], slot_send, slot_recv, where)
+        return carry
+
+    lax.fori_loop(1, 128, step_slots, 0)
+    incoming[me] = slots[me]
+    own = sources[pl.ds(me, 1), :]
+    settle(incoming.at[pl.ds(0, 127)], slot_send, slot_recv)
+    whitened[...] = place_samples(incoming, own)
+
+
+def local(panel, signs, sample_device, sample_offset):
+    shape = lambda *dims: jax.ShapeDtypeStruct(dims, F32)
+    vmem = pl.BlockSpec(memory_space=pltpu.VMEM)
+    dma = pltpu.SemaphoreType.DMA
     return pl.pallas_call(
-        body,
-        out_shape=out,
-        in_specs=[pl.BlockSpec(memory_space=pltpu.SMEM) if i in smem else spec for i in range(len(args))],
-        out_specs=jax.tree.map(lambda _: spec, out),
-        scratch_shapes=list(scratch),
-        compiler_params=pltpu.CompilerParams(vmem_limit_bytes=56 << 20),
-    )(*args)
-
-
-def shape(*dims):
-    return jax.ShapeDtypeStruct(dims, F32)
-
-
-def local(panel, signs, sample_device, sample_offset):
-    me = my_id().astype(I32).reshape(1)
-    sources = sample_device.reshape(128, 128)
-    offsets = sample_offset.reshape(128, 128)
-
-    def mix(panel_ref, signs_ref, send, table):
-        local_mix(panel_ref, signs_ref, table, send)
-
-    blocks = shape(DEVS, HALF, LANES)
-    send = call(mix, blocks, panel, signs.reshape(1, -1), scratch=[pltpu.VMEM((256, 256), BF16)])
-    arrived = lax.all_to_all(send, AXES, split_axis=0, concat_axis=0, tiled=True)
-
-    def middle(me_ref, arrived_ref, src, off, data, g, counts, acc):
-        data[...] = arrived_ref[...]
-        combine(data)
-        count_rows(src, off, counts, me_ref[0])
-        g[...] = gram(data, counts, acc)
-
-    data, g = call(
-        middle, (blocks, shape(64, 64)), me, arrived, sources, offsets,
-        scratch=[pltpu.VMEM((64, 128), F32), pltpu.VMEM((192, 192), F32)], smem=(0,),
-    )
-    back = lax.all_to_all(data, AXES, split_axis=0, concat_axis=0, tiled=True)
-    total = lax.psum(g, AXES)
-
-    def chol(g_ref, out):
-        out[...] = factor(g_ref[...] * (2.0**-34))
-
-    both = call(chol, shape(64, 128), total)
-
-    def last(me_ref, back_ref, src, off, both_ref, mixed, slots):
-        places = slot_places(src, off, me_ref[0])
-        picked = finish(back_ref, places, mixed, 2.0**-10)
-        whiten_slots(picked, both_ref[:, 64:], slots)
-
-    mixed, slots = call(
-        last, (shape(64, 8192), shape(DEVS, 2, LANES)), me, back, sources, offsets, both, smem=(0,)
-    )
-    incoming = lax.all_to_all(slots, AXES, split_axis=0, concat_axis=0, tiled=True)
-    own = lax.dynamic_slice_in_dim(sources, me[0], 1, 0)
-
-    def place(incoming_ref, own_ref, out):
-        out[...] = place_samples(incoming_ref, own_ref[...])
-
-    whitened = call(place, shape(64, 128), incoming, own)
-    return mixed, both[:, :64], whitened
+        kernel,
+        out_shape=(shape(64, 8192), shape(64, 64), shape(64, 128)),
+        in_specs=[pl.BlockSpec(memory_space=pl.ANY), vmem, vmem, vmem],
+        out_specs=(vmem, vmem, vmem),
+        scratch_shapes=[
+            pltpu.VMEM((64, 8192), F32),
+            pltpu.VMEM((256, 256), BF16),
+            pltpu.VMEM((DEVS, HALF, LANES), F32),
+            pltpu.VMEM((DEVS, HALF, LANES), F32),
+            pltpu.VMEM((DEVS, HALF, LANES), F32),
+            pltpu.VMEM((64, 128), F32),
+            pltpu.VMEM((192, 192), F32),
+            pltpu.VMEM((8, 32, 128), F32),
+            pltpu.VMEM((16, 32, 128), F32),
+            pltpu.VMEM((CAP, 64, 128), F32),
+            pltpu.VMEM((DEVS, 2, LANES), F32),
+            pltpu.VMEM((DEVS, 2, LANES), F32),
+            dma((PARTS,)), dma((PARTS,)), dma((PARTS,)), dma((PARTS,)),
+            dma, dma, dma, dma, dma, dma, dma((8,)),
+        ],
+        compiler_params=pltpu.CompilerParams(collective_id=0, has_side_effects=True, vmem_limit_bytes=56 << 20),
+    )(panel, signs.reshape(1, -1), sample_device.reshape(128, 128), sample_offset.reshape(128, 128))
 
 
 def solution(mesh):

time: 195 us -> 106 us (0.54)
  blocking collectives: 81.8 us -> 0 us
  Pallas kernels: 46.6 us -> 101 us
  waiting for transfers between devices: 39.2 us -> 0 us
  starting transfers between devices: 21.9 us -> 0 us
    psum x1 -> x0, blocking collectives: 81.8 us -> none  [local(): total = lax.psum(g, AXES)]
    pallas_call x5 -> x1, Pallas kernels: 46.6 us -> 101 us  [local(): pl.pallas_call(kernel, out_shape=(shape(64, 8192), shape(64, 64), shape(6...]
    all_to_all x3 -> x0, waiting for transfers between devices: 39.2 us -> none  [the longest x1 30.5 us: local(): lax.all_to_all(send, AXES, split_axis=0, concat_axis=0, tiled=True)]
    all_to_all x3 -> x0, starting transfers between devices: 21.9 us -> none  [the longest x1 11.5 us: local(): lax.all_to_all(send, AXES, split_axis=0, concat_axis=0, tiled=True)]
    unnamed x8 -> x7, local copies, waits for them, and re-layouts: 3.31 us -> 4.31 us
  transfers between devices with their start and end apart: 3 -> 0, of which waited for: 2 -> 0; matrix products, arithmetic and copies ran while one was open for 1% -> 0% of each run, Pallas kernels for 3% -> 0%
where the time goes in v2:
time: 106 us
  Pallas kernels  101 us (95%)
  local copies, waits for them, and re-layouts  4.31 us (4%)
    pallas_call x1, Pallas kernels, local(): pl.pallas_call(kernel, out_shape=(shape(64, 8192), shape(64, 64), shape(6...  101 us
    unnamed x7, local copies, waits for them, and re-layouts  4.31 us

profile of v2, /device:TPU:1, one launch (start us, length us, event | category | flops | bytes accessed | tf_op | source)
XLA Modules:
  0.0 106.2 jit_solution(11787755178780165882)
XLA Ops:
  0.6 101.2 %shard_map.67 = (f32[64,8192]{1,0:T(8,128)}, f32[64,64]{1,0:T(8,128)}, f32[64,128]{1,0:T(8,128)}) custom-call(f32[64,8192]{1,0:T(8,128)} %panel_hbm.1, s32[1,8192]{1,0:T(1,128)} %bitcast.5, s32[128,128]{1,0:T(8,128)} %bitcast.3, s32[128,128]{1,0:T(8,128)} %bitcast.4), custom_call_target="tpu_custom_call" | custom-call | tf_op jit(solution)/shard_map/pallas_call | solution.py:410
  101.9 0.0 copy-start.1
  101.9 0.0 copy-start
  101.9 3.1 %copy.10 = f32[64,8192]{1,0:T(8,128)} copy(f32[64,8192]{1,0:T(8,128)} %get-tuple-element.6) | data formatting | bytes 4194304
  105.0 0.0 copy-done.1
  105.0 0.6 copy.11
  105.6 0.0 copy-done
  105.6 0.6 copy.12
Async XLA Ops:
  101.9 3.1 %copy-start.1 = (f32[64,64]{1,0:T(8,128)S(1)}, f32[64,64]{1,0:T(8,128)}, u32[]{:S(2)}) copy-start(f32[64,64]{1,0:T(8,128)} %get-tuple-element.7) | copy-start | bytes 49156
  101.9 3.7 %copy-start = (f32[64,128]{1,0:T(8,128)S(1)}, f32[64,128]{1,0:T(8,128)}, u32[]{:S(2)}) copy-start(f32[64,128]{1,0:T(8,128)} %get-tuple-element.8) | copy-start | bytes 98308

commit v3 on v2

--- a/solution.py
+++ b/solution.py
@@ -53,7 +53,7 @@
         bits = jnp.bitwise_xor(bits, lax.shift_right_logical(bits, shift))
     sign = 1.0 - 2.0 * jnp.bitwise_and(bits, 1).astype(F32)
     return jnp.where(k // 128 == (n % 128) // 64, sign, 0.0).astype(BF16)
-SPLIT = 72
+HELD, AHEAD = 105, 50
 
 
 PARTS = 2
@@ -117,13 +117,6 @@
     lax.fori_loop(0, 16, second, 0)
 
 
-def unpack(a, b):
-    left = iota((HALF, LANES), 1) < 64
-    upper = jnp.where(left, a, pltpu.roll(b, 64, 1))
-    lower = jnp.where(left, pltpu.roll(a, 64, 1), b)
-    return jnp.concatenate([upper, lower], axis=0)
-
-
 def count_rows(sources, offsets, counts, me):
     counts[...] = jnp.zeros_like(counts)
 
@@ -144,24 +137,66 @@
         return carry
 
     lax.fori_loop(0, 16, step, 0)
-
-
-def gram(data, counts, acc):
+    counts[...] = jnp.sqrt(counts[...])
+
+
+def weighted_parts(part, data, roots, i):
+    left = iota((ROWS, LANES), 1) < 64
+    pieces = []
+    for q in (2 * i, 2 * i + 1):
+        one, two = data[q, pl.ds(part * ROWS, ROWS)], data[q + 64, pl.ds(part * ROWS, ROWS)]
+        upper = jnp.where(left, one, pltpu.roll(two, 64, 1))
+        lower = jnp.where(left, pltpu.roll(one, 64, 1), two)
+        pieces.append(jnp.concatenate([upper, lower], axis=0) * roots[pl.ds(q, 1), :])
+    return jnp.concatenate(split3(jnp.concatenate(pieces, axis=1)), axis=0)
+
+
+def gram_first(data, roots, parts, acc):
     acc[...] = jnp.zeros_like(acc)
 
     def step(i, carry):
-        x = jnp.concatenate([unpack(data[2 * i], data[2 * i + 64]), unpack(data[2 * i + 1], data[2 * i + 65])], axis=1)
-        w = jnp.concatenate([counts[pl.ds(2 * i, 1), :], counts[pl.ds(2 * i + 1, 1), :]], axis=1)
-        plain = jnp.concatenate(split3(x), axis=0)
-        weighted = jnp.concatenate(split3(x * w), axis=0)
-        acc[...] += dot_nt(weighted, plain)
-        return carry
-
-    lax.fori_loop(0, 32, step, 0)
-    block = lambda i, j: acc[64 * i : 64 * i + 64, 64 * j : 64 * j + 64]
+        total = acc[...]
+        for k in range(4):
+            own = weighted_parts(0, data, roots, 4 * i + k)
+            parts[4 * i + k] = own
+            total = total + dot_nt(own, own)
+        acc[...] = total
+        return carry
+
+    lax.fori_loop(0, 8, step, 0)
+
+
+def gram_second(data, roots, parts, acc):
+    acc[...] = jnp.zeros_like(acc)
+
+    def step(i, carry):
+        total = acc[...]
+        for k in range(4):
+            own = weighted_parts(1, data, roots, 4 * i + k)
+            total = total + dot_nt(jnp.concatenate([parts[4 * i + k], own], axis=0), own)
+        acc[...] = total
+        return carry
+
+    lax.fori_loop(0, 8, step, 0)
+
+
+def merge_parts(acc, row):
+    block = lambda i, j: acc[row + 32 * i : row + 32 * i + 32, 32 * j : 32 * j + 32]
     small = block(2, 2) + (block(1, 2) + block(2, 1))
     small = small + (block(0, 2) + block(2, 0)) + block(1, 1)
     return small + (block(0, 1) + block(1, 0)) + block(0, 0)
+
+
+def gram(first, second):
+    same, cross, last = merge_parts(first, 0), merge_parts(second, 0), merge_parts(second, 96)
+    g = jnp.concatenate(
+        [jnp.concatenate([same, cross], axis=1), jnp.concatenate([cross.T, last], axis=1)], axis=0
+    )
+    swap = lambda m, dim: jnp.concatenate(
+        [lax.slice_in_dim(m, at, at + 16, axis=dim) for at in (0, 32, 16, 48)], axis=dim
+    )
+    g = swap(swap(g, 0), 1)
+    return jnp.concatenate([g[:32], g[32:]], axis=1)
 
 
 def factor(g):
@@ -198,40 +233,44 @@
 
 
 def unpack_part(part, back, mixed, scale):
-    def step(b, carry):
-        at = pl.ds(pl.multiple_of(b * 128, 128), 128)
-        one, two = back[2 * b, pl.ds(part * ROWS, ROWS)], back[2 * b + 1, pl.ds(part * ROWS, ROWS)]
-        left = iota((ROWS, LANES), 1) < 64
-        mixed[part * ROWS : part * ROWS + ROWS, at] = jnp.where(left, one, pltpu.roll(two, 64, 1)) * scale
-        mixed[HALF + part * ROWS : HALF + part * ROWS + ROWS, at] = jnp.where(left, pltpu.roll(one, 64, 1), two) * scale
-        return carry
-
-    lax.fori_loop(0, 64, step, 0)
+    left = iota((ROWS, LANES), 1) < 64
+
+    def step(i, carry):
+        for k in range(8):
+            b = 8 * i + k
+            at = pl.ds(pl.multiple_of(b * 128, 128), 128)
+            one, two = back[2 * b, pl.ds(part * ROWS, ROWS)], back[2 * b + 1, pl.ds(part * ROWS, ROWS)]
+            upper = jnp.where(left, one, pltpu.roll(two, 64, 1))
+            lower = jnp.where(left, pltpu.roll(one, 64, 1), two)
+            mixed[part * ROWS : part * ROWS + ROWS, at] = upper * scale
+            mixed[HALF + part * ROWS : HALF + part * ROWS + ROWS, at] = lower * scale
+        return carry
+
+    lax.fori_loop(0, 8, step, 0)
 
 
 def pick_part(part, mixed, places, picked):
+    bases = [half + part * ROWS + 8 * k for half in (0, HALF) for k in range(ROWS // 8)]
     for r, (high, low) in enumerate(places):
-        high = jnp.concatenate([high] * (ROWS // 8), axis=0)
-        low = jnp.concatenate([low] * (ROWS // 8), axis=0)
 
         def step(i, found):
-            for k in range(4):
-                b = 4 * i + k
+            for k in range(16):
+                b = 16 * i + k
                 at = pl.ds(pl.multiple_of(b * 128, 128), 128)
+                here = high == b
                 found = tuple(
                     jnp.where(
-                        high == b,
-                        jnp.take_along_axis(mixed[base : base + ROWS, at], low, axis=1, mode="promise_in_bounds"),
+                        here,
+                        jnp.take_along_axis(mixed[base : base + 8, at], low, axis=1, mode="promise_in_bounds"),
                         old,
                     )
-                    for base, old in zip((part * ROWS, HALF + part * ROWS), found)
+                    for base, old in zip(bases, found)
                 )
             return found
 
-        zero = jnp.zeros((ROWS, LANES), F32)
-        upper, lower = lax.fori_loop(0, 16, step, (zero, zero))
-        picked[r, part * ROWS : part * ROWS + ROWS] = upper
-        picked[r, HALF + part * ROWS : HALF + part * ROWS + ROWS] = lower
+        done = lax.fori_loop(0, 4, step, tuple(jnp.zeros((8, LANES), F32) for _ in bases))
+        for base, value in zip(bases, done):
+            picked[r, base : base + 8] = value
 
 
 def exact6(a, b, dot):
@@ -244,7 +283,7 @@
 def whiten_slots(picked, inverse, out):
     done = [exact6(p.T, inverse, dot_nt) for p in picked]
     for pair in range(2):
-        out[:, pair, :] = jnp.concatenate(done[2 * pair : 2 * pair + 2], axis=1)
+        out[:, :, pair, :] = jnp.concatenate(done[2 * pair : 2 * pair + 2], axis=1).reshape(16, 8, LANES)
 
 
 def place_samples(incoming, own):
@@ -253,7 +292,7 @@
     rank = dot_nn(flag.astype(BF16), earlier())
     total = jnp.zeros((COLS, LANES), F32)
     for pair in range(2):
-        top, mid, low = split3(incoming[:, pair, :])
+        top, mid, low = split3(incoming[:, :, pair, :].reshape(DEVS, LANES))
         for half in range(2):
             chosen = jnp.where(rank == float(2 * pair + half), flag, 0.0).astype(BF16)
             got = dot_tn(low, chosen) + dot_tn(mid, chosen) + dot_tn(top, chosen)
@@ -274,11 +313,36 @@
     return ((z * 4 + x) * 2 + c) * 4 + y
 
 
-def peer(t):
+def in_line(t):
     z, x, c, y = position()
-    u = t // 2
-    a, b, e = u % 4, (u // 4) % 4, u // 16
-    return (z + a + 2 * b + e) % 4, (x + a + b) % 4, (c + t) % 2, (y + a) % 4
+    return z, x, (c + t) % 2, (y + t // 2) % 4
+
+
+def in_plane(t):
+    z, x, c, y = position()
+    return (z + t // 4 + t) % 4, (x + t) % 4, c, y
+
+
+def elsewhere(i):
+    z, x, _, _ = in_plane(1 + i % 15)
+    _, _, c, y = in_line(1 + i % 7)
+    return z, x, c, y
+
+
+def run(low, high, step):
+    whole = (high - low) // 7
+
+    def several(i, carry):
+        for k in range(7):
+            step(low + 7 * i + k, 0)
+        return carry
+
+    lax.fori_loop(0, whole, several, 0)
+    for t in range(low + 7 * whole, high):
+        step(t, 0)
+
+
+GROUPS = ((in_line, 1, 8), (in_plane, 1, 16), (elsewhere, 0, 105))
 
 
 def start(src, dst, send_sem, recv_sem, where):
@@ -289,16 +353,17 @@
 
 def settle(ref, send_sem, recv_sem):
     whole = pltpu.make_async_remote_copy(
-        src_ref=ref, dst_ref=ref, send_sem=send_sem, recv_sem=recv_sem, device_id=device(*peer(1)), device_id_type=MESH
+        src_ref=ref, dst_ref=ref, send_sem=send_sem, recv_sem=recv_sem, device_id=device(*in_line(1)), device_id_type=MESH
     )
     whole.wait_recv()
     whole.wait_send()
 
 
 def kernel(
-    panel_hbm, signs, sources, offsets, mixed, factor_out, whitened,
-    panel, table, send, arrived, back, counts, acc, first_sums, second_sums, picked, slots, incoming,
-    out_send, out_recv, back_send, back_recv, one_send, one_recv, two_send, two_recv, slot_send, slot_recv, load_sem,
+    panel_hbm, signs_hbm, sources_hbm, offsets_hbm, mixed, factor_out, whitened,
+    panel, signs, sources, offsets, table, send, arrived, back, counts, parts, acc, acc2, first_sums, second_sums, picked, slots, relay, incoming,
+    out_send, out_recv, back_send, back_recv, one_send, one_recv, two_send, two_recv,
+    line_send, line_recv, plane_send, plane_recv, load_sem, ready,
 ):
     z, x, c, y = position()
     me = flat(z, x, c, y)
@@ -306,74 +371,92 @@
     loads = [
         pltpu.make_async_copy(panel_hbm.at[pl.ds(8 * g, 8)], panel.at[pl.ds(8 * g, 8)], load_sem.at[g]) for g in range(8)
     ]
-    for load in loads:
+    tables = [
+        pltpu.make_async_copy(src, dst, load_sem.at[8 + i])
+        for i, (src, dst) in enumerate(((signs_hbm, signs), (sources_hbm, sources), (offsets_hbm, offsets)))
+    ]
+    for load in tables[:1] + loads + tables[1:]:
         load.start()
 
-    def greet(t, carry):
-        pl.semaphore_signal(barrier, inc=1, device_id=device(*peer(t)), device_id_type=MESH)
-        return carry
-
-    lax.fori_loop(1, 128, greet, 0)
+    def signal_all(sem, peers, count):
+        def step(t, carry):
+            pl.semaphore_signal(sem, inc=1, device_id=device(*peers(t)), device_id_type=MESH)
+            return carry
+
+        lax.fori_loop(1, count, step, 0)
+
+    signal_all(barrier, in_line, 8)
+    signal_all(barrier, in_plane, 16)
     table[...] = lane_table()
     rows = lambda part: pl.ds(part * ROWS, ROWS)
 
-    def send_out(part):
-        def step(t, carry):
-            where = peer(t)
-            start(send.at[flat(*where), rows(part)], arrived.at[me, rows(part)], out_send.at[part], out_recv.at[part], where)
-            return carry
-
-        lax.fori_loop(1, 128, step, 0)
-        arrived[me, rows(part)] = send[me, rows(part)]
-
-    def send_back(part, low, high):
-        def step(t, carry):
-            where = peer(t)
-            start(arrived.at[flat(*where), rows(part)], back.at[me, rows(part)], back_send.at[part], back_recv.at[part], where)
-            return carry
-
-        lax.fori_loop(low, high, step, 0)
-
+    def send_out(part, groups):
+        for group, low, high in groups:
+
+            def step(t, carry):
+                where = group(t)
+                start(send.at[flat(*where), rows(part)], arrived.at[me, rows(part)], out_send.at[part], out_recv.at[part], where)
+                return carry
+
+            run(low, high, step)
+
+    def send_back(part, groups):
+        for group, low, high in groups:
+
+            def step(t, carry):
+                where = group(t)
+                start(arrived.at[flat(*where), rows(part)], back.at[me, rows(part)], back_send.at[part], back_recv.at[part], where)
+                return carry
+
+            run(low, high, step)
+
+    tables[0].wait()
     for part in range(PARTS):
         for g in range(8):
             if (g % 4) * 8 // ROWS == part:
                 loads[g].wait()
         local_mix(part, panel, signs, table, send)
         if part == 0:
-            pl.semaphore_wait(barrier, 127)
-        send_out(part)
+            pl.semaphore_wait(barrier, 22)
+            signal_all(ready, in_plane, 16)
+        send_out(part, GROUPS[:2])
+    pl.semaphore_wait(ready, 15)
+    for part in range(PARTS):
+        send_out(part, GROUPS[2:])
+        arrived[me, rows(part)] = send[me, rows(part)]
+    tables[1].wait()
+    tables[2].wait()
     count_rows(sources, offsets, counts, me)
     places = slot_places(sources, offsets, me)
     for part in range(PARTS):
         settle(arrived.at[pl.ds(0, 127), rows(part)], out_send.at[part], out_recv.at[part])
         combine(part, arrived)
-        send_back(part, 1, 128 if part < PARTS - 1 else SPLIT)
+        if part == 0:
+            send_back(0, ((elsewhere, 0, HELD),))
         back[me, rows(part)] = arrived[me, rows(part)]
-
-    g = gram(arrived, counts, acc)
-    mine = c * 4 + y
-    first_sums[mine] = jnp.concatenate([g[:32], g[32:]], axis=1)
-
-    def step_one(t, carry):
-        where = (z, x, (c + t) % 2, (y + t // 2) % 4)
-        start(first_sums.at[mine], first_sums.at[mine], one_send, one_recv, where)
-        return carry
-
-    lax.fori_loop(1, 8, step_one, 0)
-    send_back(PARTS - 1, SPLIT, 128)
+        if part == 0:
+            gram_first(arrived, counts, parts, acc)
+    gram_second(arrived, counts, parts, acc2)
+    line, plane = c * 4 + y, z * 4 + x
+    first_sums[line] = gram(acc, acc2)
+
+    def send_sums(sums, at, peers, count, send_sem, recv_sem):
+        def step(t, carry):
+            start(sums.at[at], sums.at[at], send_sem, recv_sem, peers(t))
+            return carry
+
+        lax.fori_loop(1, count, step, 0)
+
+    send_sums(first_sums, line, in_line, 8, one_send, one_recv)
+    send_back(0, ((elsewhere, HELD, 105),) + GROUPS[:2])
+    send_back(1, ((elsewhere, 0, AHEAD),))
     settle(first_sums.at[pl.ds(0, 7)], one_send, one_recv)
     total = first_sums[0]
     for i in range(1, 8):
         total = total + first_sums[i]
-    line = z * 4 + x
-    second_sums[line] = total
-
-    def step_two(t, carry):
-        where = ((z + t // 4) % 4, (x + t) % 4, c, y)
-        start(second_sums.at[line], second_sums.at[line], two_send, two_recv, where)
-        return carry
-
-    lax.fori_loop(1, 16, step_two, 0)
+    second_sums[plane] = total
+    send_sums(second_sums, plane, in_plane, 16, two_send, two_recv)
+    send_back(1, ((elsewhere, AHEAD, 105),) + GROUPS[:2])
     for part in range(PARTS - 1):
         settle(back.at[pl.ds(0, 127), rows(part)], back_send.at[part], back_recv.at[part])
         unpack_part(part, back, mixed, 2.0**-10)
@@ -391,45 +474,79 @@
     pick_part(last, mixed, places, picked)
     whiten_slots([picked[r] for r in range(CAP)], both[:, 64:], slots)
 
-    def step_slots(t, carry):
-        where = peer(t)
-        start(slots.at[flat(*where)], incoming.at[me], slot_send, slot_recv, where)
-        return carry
-
-    lax.fori_loop(1, 128, step_slots, 0)
-    incoming[me] = slots[me]
+    def step_line(t, carry):
+        _, _, pc, py = where = in_line(t)
+        start(slots.at[:, pc * 4 + py], relay.at[line], line_send, line_recv, where)
+        return carry
+
+    lax.fori_loop(1, 8, step_line, 0)
+    relay[line] = slots[:, line]
     own = sources[pl.ds(me, 1), :]
-    settle(incoming.at[pl.ds(0, 127)], slot_send, slot_recv)
+    settle(relay.at[pl.ds(0, 7)], line_send, line_recv)
+
+    def step_plane(t, carry):
+        pz, px, _, _ = where = in_plane(t)
+        start(relay.at[:, pz * 4 + px], incoming.at[plane], plane_send, plane_recv, where)
+        return carry
+
+    lax.fori_loop(1, 16, step_plane, 0)
+    incoming[plane] = relay[:, plane]
+    settle(incoming.at[pl.ds(0, 15)], plane_send, plane_recv)
     whitened[...] = place_samples(incoming, own)
+
+
+def pass_on(mixed_in, factor_in, whitened_in, mixed, factor_out, whitened, sems):
+    pairs = [(mixed_in.at[pl.ds(8 * g, 8)], mixed.at[pl.ds(8 * g, 8)]) for g in range(8)]
+    pairs += [(factor_in, factor_out), (whitened_in, whitened)]
+    copies = [pltpu.make_async_copy(src, dst, sems.at[i]) for i, (src, dst) in enumerate(pairs)]
+    for copy in copies:
+        copy.start()
+    for copy in copies:
+        copy.wait()
 
 
 def local(panel, signs, sample_device, sample_offset):
     shape = lambda *dims: jax.ShapeDtypeStruct(dims, F32)
     vmem = pl.BlockSpec(memory_space=pltpu.VMEM)
     dma = pltpu.SemaphoreType.DMA
-    return pl.pallas_call(
+    made = pl.pallas_call(
         kernel,
         out_shape=(shape(64, 8192), shape(64, 64), shape(64, 128)),
-        in_specs=[pl.BlockSpec(memory_space=pl.ANY), vmem, vmem, vmem],
+        in_specs=[pl.BlockSpec(memory_space=pltpu.HBM)] * 4,
         out_specs=(vmem, vmem, vmem),
         scratch_shapes=[
             pltpu.VMEM((64, 8192), F32),
+            pltpu.VMEM((1, 8192), I32),
+            pltpu.VMEM((128, 128), I32),
+            pltpu.VMEM((128, 128), I32),
             pltpu.VMEM((256, 256), BF16),
             pltpu.VMEM((DEVS, HALF, LANES), F32),
             pltpu.VMEM((DEVS, HALF, LANES), F32),
             pltpu.VMEM((DEVS, HALF, LANES), F32),
             pltpu.VMEM((64, 128), F32),
-            pltpu.VMEM((192, 192), F32),
+            pltpu.VMEM((32, 96, 256), BF16),
+            pltpu.VMEM((96, 96), F32),
+            pltpu.VMEM((192, 96), F32),
             pltpu.VMEM((8, 32, 128), F32),
             pltpu.VMEM((16, 32, 128), F32),
             pltpu.VMEM((CAP, 64, 128), F32),
-            pltpu.VMEM((DEVS, 2, LANES), F32),
-            pltpu.VMEM((DEVS, 2, LANES), F32),
+            pltpu.VMEM((16, 8, 2, LANES), F32),
+            pltpu.VMEM((8, 16, 2, LANES), F32),
+            pltpu.VMEM((16, 8, 2, LANES), F32),
             dma((PARTS,)), dma((PARTS,)), dma((PARTS,)), dma((PARTS,)),
-            dma, dma, dma, dma, dma, dma, dma((8,)),
+            dma, dma, dma, dma, dma, dma, dma, dma, dma((11,)), pltpu.SemaphoreType.REGULAR,
         ],
-        compiler_params=pltpu.CompilerParams(collective_id=0, has_side_effects=True, vmem_limit_bytes=56 << 20),
-    )(panel, signs.reshape(1, -1), sample_device.reshape(128, 128), sample_offset.reshape(128, 128))
+        compiler_params=pltpu.CompilerParams(collective_id=0, has_side_effects=True, vmem_limit_bytes=20 << 20),
+    )(*(pltpu.with_memory_space_constraint(v, pltpu.HBM) for v in (panel, signs.reshape(1, -1), sample_device.reshape(128, 128), sample_offset.reshape(128, 128))))
+    anywhere = pl.BlockSpec(memory_space=pl.ANY)
+    return pl.pallas_call(
+        pass_on,
+        out_shape=(shape(64, 8192), shape(64, 64), shape(64, 128)),
+        in_specs=[vmem, vmem, vmem],
+        out_specs=(anywhere, anywhere, anywhere),
+        scratch_shapes=[dma((10,))],
+        compiler_params=pltpu.CompilerParams(vmem_limit_bytes=8 << 20),
+    )(*made)
 
 
 def solution(mesh):

time: 106 us -> 84 us (0.79)
  Pallas kernels: 101 us -> 83.2 us
  local copies, waits for them, and re-layouts: 4.31 us -> 0 us
    pallas_call x1, Pallas kernels: 101 us -> 81.8 us  [local(): pl.pallas_call(kernel, out_shape=(shape(64, 8192), shape(64, 64), shape(6...]
    unnamed x7 -> x0, local copies, waits for them, and re-layouts: 4.31 us -> none
    pallas_call x0 -> x1, Pallas kernels: none -> 1.4 us  [local(): pl.pallas_call(pass_on, out_shape=(shape(64, 8192), shape(64, 64), shape(...]
where the time goes in v3:
time: 84 us; the launch traced here: 83.8 us
  Pallas kernels  83.2 us (99%)
    pallas_call x1, Pallas kernels, local(): pl.pallas_call(kernel, out_shape=(shape(64, 8192), shape(64, 64), shape(6...  81.8 us

profile of v3, /device:TPU:1, one launch (start us, length us, event | category | flops | bytes accessed | tf_op | source)
XLA Modules:
  0.0 83.8 jit_solution(1044708157140933192)
XLA Ops:
  0.6 81.8 %shard_map.67 = (f32[64,8192]{1,0:T(8,128)S(1)}, f32[64,64]{1,0:T(8,128)S(1)}, f32[64,128]{1,0:T(8,128)S(1)}) custom-call(f32[64,8192]{1,0:T(8,128)} %panel_hbm.1, s32[1,8192]{1,0:T(1,128)} %bitcast.5, s32[128,128]{1,0:T(8,128)} %bitcast.3, s32[128,128]{1,0:T(8,128)} %bitcast.4), custom_call_target="tpu_custom_call" | custom-call | tf_op jit(solution)/shard_map/pallas_call | solution.py:512
  82.4 1.4 %shard_map.68 = (f32[64,8192]{1,0:T(8,128)}, f32[64,64]{1,0:T(8,128)}, f32[64,128]{1,0:T(8,128)}) custom-call(f32[64,8192]{1,0:T(8,128)S(1)} %get-tuple-element.6.mixed_in, f32[64,64]{1,0:T(8,128)S(1)} %get-tuple-element.7.factor_in, f32[64,128]{1,0:T(8,128)S(1)} %get-tuple-element.8.whitened_in), custom_call_target="tpu_custom_call" | custom-call | tf_op jit(solution)/shard_map/pallas_call | solution.py:542

commit v4 on v3

--- a/solution.py
+++ b/solution.py
@@ -53,7 +53,7 @@
         bits = jnp.bitwise_xor(bits, lax.shift_right_logical(bits, shift))
     sign = 1.0 - 2.0 * jnp.bitwise_and(bits, 1).astype(F32)
     return jnp.where(k // 128 == (n % 128) // 64, sign, 0.0).astype(BF16)
-HELD, AHEAD = 105, 50
+MIDDLE = 24
 
 
 PARTS = 2
@@ -199,15 +199,22 @@
     return jnp.concatenate([g[:32], g[32:]], axis=1)
 
 
-def factor(g):
-    sub, lane = iota((COLS, LANES), 0), iota((COLS, LANES), 1)
-    m = jnp.concatenate([g, jnp.where(sub == lane, 1.0, 0.0)[:, :64]], axis=1)
+def bordered(g):
+    return jnp.concatenate([g, jnp.where(iota((COLS, 64), 0) == iota((COLS, 64), 1), 1.0, 0.0)], axis=1)
+
+
+def eliminate(m, low, high):
     subs = iota((COLS, 1), 0)
-    for j in range(COLS):
+    for j in range(low, high):
         pivot_row = m[j : j + 1, :]
         inverse = 1.0 / m[j : j + 1, j : j + 1]
         lead = jnp.where(subs > j, m[:, j : j + 1] * inverse, 0.0)
         m = m - lead * pivot_row
+    return m
+
+
+def factors(m):
+    sub, lane = iota((COLS, LANES), 0), iota((COLS, LANES), 1)
     diagonal = jnp.sum(jnp.where(sub == lane, m, 0.0), axis=1, keepdims=True)
     scaled = m / jnp.sqrt(diagonal)
     return jnp.where(jnp.logical_or(lane >= sub, lane >= 64), scaled, 0.0)
@@ -280,10 +287,10 @@
     return small + (dot(a1, b2) + dot(a2, b1)) + dot(a1, b1)
 
 
-def whiten_slots(picked, inverse, out):
-    done = [exact6(p.T, inverse, dot_nt) for p in picked]
+def pack_slots(picked, out):
     for pair in range(2):
-        out[:, :, pair, :] = jnp.concatenate(done[2 * pair : 2 * pair + 2], axis=1).reshape(16, 8, LANES)
+        both = jnp.concatenate([picked[2 * pair].T, picked[2 * pair + 1].T], axis=1)
+        out[:, :, pair, :] = both.reshape(16, 8, LANES)
 
 
 def place_samples(incoming, own):
@@ -432,7 +439,9 @@
         settle(arrived.at[pl.ds(0, 127), rows(part)], out_send.at[part], out_recv.at[part])
         combine(part, arrived)
         if part == 0:
-            send_back(0, ((elsewhere, 0, HELD),))
+            send_back(0, GROUPS[2:] + GROUPS[:2])
+        else:
+            send_back(1, ((elsewhere, 0, 49),))
         back[me, rows(part)] = arrived[me, rows(part)]
         if part == 0:
             gram_first(arrived, counts, parts, acc)
@@ -448,40 +457,36 @@
         lax.fori_loop(1, count, step, 0)
 
     send_sums(first_sums, line, in_line, 8, one_send, one_recv)
-    send_back(0, ((elsewhere, HELD, 105),) + GROUPS[:2])
-    send_back(1, ((elsewhere, 0, AHEAD),))
+    send_back(1, ((elsewhere, 49, 105),) + GROUPS[:2])
+    for part in range(PARTS - 1):
+        settle(back.at[pl.ds(0, 127), rows(part)], back_send.at[part], back_recv.at[part])
+        unpack_part(part, back, mixed, 2.0**-10)
+        pick_part(part, mixed, places, picked)
     settle(first_sums.at[pl.ds(0, 7)], one_send, one_recv)
     total = first_sums[0]
     for i in range(1, 8):
         total = total + first_sums[i]
     second_sums[plane] = total
     send_sums(second_sums, plane, in_plane, 16, two_send, two_recv)
-    send_back(1, ((elsewhere, AHEAD, 105),) + GROUPS[:2])
-    for part in range(PARTS - 1):
-        settle(back.at[pl.ds(0, 127), rows(part)], back_send.at[part], back_recv.at[part])
-        unpack_part(part, back, mixed, 2.0**-10)
-        pick_part(part, mixed, places, picked)
+    last = PARTS - 1
+    settle(back.at[pl.ds(0, 127), rows(last)], back_send.at[last], back_recv.at[last])
+    unpack_part(last, back, mixed, 2.0**-10)
+    pick_part(last, mixed, places, picked)
+    pack_slots([picked[r] for r in range(CAP)], slots)
+
+    def step_line(t, carry):
+        _, _, pc, py = where = in_line(t)
+        start(slots.at[:, pc * 4 + py], relay.at[line], line_send, line_recv, where)
+        return carry
+
+    lax.fori_loop(1, 8, step_line, 0)
+    relay[line] = slots[:, line]
+    own = sources[pl.ds(me, 1), :]
     settle(second_sums.at[pl.ds(0, 15)], two_send, two_recv)
     total = second_sums[0]
     for i in range(1, 16):
         total = total + second_sums[i]
-    both = factor(jnp.concatenate([total[:, :64], total[:, 64:]], axis=0) * (2.0**-34))
-    factor_out[...] = both[:, :64]
-
-    last = PARTS - 1
-    settle(back.at[pl.ds(0, 127), rows(last)], back_send.at[last], back_recv.at[last])
-    unpack_part(last, back, mixed, 2.0**-10)
-    pick_part(last, mixed, places, picked)
-    whiten_slots([picked[r] for r in range(CAP)], both[:, 64:], slots)
-
-    def step_line(t, carry):
-        _, _, pc, py = where = in_line(t)
-        start(slots.at[:, pc * 4 + py], relay.at[line], line_send, line_recv, where)
-        return carry
-
-    lax.fori_loop(1, 8, step_line, 0)
-    relay[line] = slots[:, line]
-    own = sources[pl.ds(me, 1), :]
+    state = eliminate(bordered(jnp.concatenate([total[:, :64], total[:, 64:]], axis=0) * (2.0**-34)), 0, MIDDLE)
     settle(relay.at[pl.ds(0, 7)], line_send, line_recv)
 
     def step_plane(t, carry):
@@ -491,8 +496,10 @@
 
     lax.fori_loop(1, 16, step_plane, 0)
     incoming[plane] = relay[:, plane]
+    both = factors(eliminate(state, MIDDLE, COLS))
+    factor_out[...] = both[:, :64]
     settle(incoming.at[pl.ds(0, 15)], plane_send, plane_recv)
-    whitened[...] = place_samples(incoming, own)
+    whitened[...] = exact6(both[:, 64:], place_samples(incoming, own), dot_nn)
 
 
 def pass_on(mixed_in, factor_in, whitened_in, mixed, factor_out, whitened, sems):

time: 84 us -> 75.6 us (0.90)
  Pallas kernels: 83.2 us -> 74.9 us
    pallas_call x1, Pallas kernels: 81.8 us -> 73.5 us  [local(): pl.pallas_call(kernel, out_shape=(shape(64, 8192), shape(64, 64), shape(6...]
where the time goes in v4:
time: 75.6 us; the launch traced here: 75.5 us
  Pallas kernels  74.9 us (99%)
    pallas_call x1, Pallas kernels, local(): pl.pallas_call(kernel, out_shape=(shape(64, 8192), shape(64, 64), shape(6...  73.5 us

profile of v4, /device:TPU:1, one launch (start us, length us, event | category | flops | bytes accessed | tf_op | source)
XLA Modules:
  0.0 75.5 jit_solution(8432469558256790964)
XLA Ops:
  0.6 73.5 %shard_map.67 = (f32[64,8192]{1,0:T(8,128)S(1)}, f32[64,64]{1,0:T(8,128)S(1)}, f32[64,128]{1,0:T(8,128)S(1)}) custom-call(f32[64,8192]{1,0:T(8,128)} %panel_hbm.1, s32[1,8192]{1,0:T(1,128)} %bitcast.5, s32[128,128]{1,0:T(8,128)} %bitcast.3, s32[128,128]{1,0:T(8,128)} %bitcast.4), custom_call_target="tpu_custom_call" | custom-call | tf_op jit(solution)/shard_map/pallas_call | solution.py:519
  74.1 1.4 %shard_map.68 = (f32[64,8192]{1,0:T(8,128)}, f32[64,64]{1,0:T(8,128)}, f32[64,128]{1,0:T(8,128)}) custom-call(f32[64,8192]{1,0:T(8,128)S(1)} %get-tuple-element.6.mixed_in, f32[64,64]{1,0:T(8,128)S(1)} %get-tuple-element.7.factor_in, f32[64,128]{1,0:T(8,128)S(1)} %get-tuple-element.8.whitened_in), custom_call_target="tpu_custom_call" | custom-call | tf_op jit(solution)/shard_map/pallas_call | solution.py:549

commit v5 on v4

--- a/solution.py
+++ b/solution.py
@@ -53,22 +53,23 @@
         bits = jnp.bitwise_xor(bits, lax.shift_right_logical(bits, shift))
     sign = 1.0 - 2.0 * jnp.bitwise_and(bits, 1).astype(F32)
     return jnp.where(k // 128 == (n % 128) // 64, sign, 0.0).astype(BF16)
-MIDDLE = 24
+MIDDLE = 16
 
 
 PARTS = 2
-ROWS = HALF // PARTS
+LOWS, SIZES = (0, 16), (16, 16)
 MESH = pl.DeviceIdType.MESH
 
 
 def local_mix(part, panel, signs, table, send):
-    at_rows = pl.ds(part * ROWS, ROWS)
+    base, size = LOWS[part], SIZES[part]
+    at_rows = pl.ds(base, size)
 
     def first(high, carry):
         at = pl.ds(pl.multiple_of(high * 1024, 1024), 1024)
         sign = signs[:, at].astype(F32)
-        upper = panel[part * ROWS : part * ROWS + ROWS, at] * sign
-        lower = panel[HALF + part * ROWS : HALF + part * ROWS + ROWS, at] * sign
+        upper = panel[base : base + size, at] * sign
+        lower = panel[HALF + base : HALF + base + size, at] * sign
         lhs = jnp.concatenate(
             [
                 jnp.concatenate([upper[:, 128 * b : 128 * b + 128], lower[:, 128 * b : 128 * b + 128]], axis=1)
@@ -79,7 +80,7 @@
         weights = table[...]
         top, mid, low = split3(lhs)
         out = dot_nn(low, weights) + dot_nn(mid, weights) + dot_nn(top, weights)
-        done = butterflies([out[ROWS * b : ROWS * b + ROWS] for b in range(8)])
+        done = butterflies([out[size * b : size * b + size] for b in range(8)])
         for b in range(8):
             send[16 * high + 2 * b, at_rows] = done[b][:, :128]
             send[16 * high + 2 * b + 1, at_rows] = done[b][:, 128:]
@@ -97,16 +98,18 @@
 
 
 def combine(part, data):
+    base, size = LOWS[part], SIZES[part]
+
     def first(i, carry):
-        high, group = i // (ROWS // 8), i % (ROWS // 8)
-        at = pl.ds(pl.multiple_of(part * ROWS + group * 8, 8), 8)
+        high, group = i // (size // 8), i % (size // 8)
+        at = pl.ds(pl.multiple_of(base + group * 8, 8), 8)
         done = butterflies([data[16 * high + low, at] for low in range(16)])
         for low in range(16):
             data[16 * high + low, at] = done[low]
         return carry
 
-    lax.fori_loop(0, 8 * (ROWS // 8), first, 0)
-    at_rows = pl.ds(part * ROWS, ROWS)
+    lax.fori_loop(0, size, first, 0)
+    at_rows = pl.ds(base, size)
 
     def second(low, carry):
         done = butterflies([data[16 * high + low, at_rows] for high in range(8)])
@@ -141,10 +144,11 @@
 
 
 def weighted_parts(part, data, roots, i):
-    left = iota((ROWS, LANES), 1) < 64
+    base, size = LOWS[part], SIZES[part]
+    left = iota((size, LANES), 1) < 64
     pieces = []
     for q in (2 * i, 2 * i + 1):
-        one, two = data[q, pl.ds(part * ROWS, ROWS)], data[q + 64, pl.ds(part * ROWS, ROWS)]
+        one, two = data[q, pl.ds(base, size)], data[q + 64, pl.ds(base, size)]
         upper = jnp.where(left, one, pltpu.roll(two, 64, 1))
         lower = jnp.where(left, pltpu.roll(one, 64, 1), two)
         pieces.append(jnp.concatenate([upper, lower], axis=0) * roots[pl.ds(q, 1), :])
@@ -180,21 +184,21 @@
     lax.fori_loop(0, 8, step, 0)
 
 
-def merge_parts(acc, row):
-    block = lambda i, j: acc[row + 32 * i : row + 32 * i + 32, 32 * j : 32 * j + 32]
+def merge_parts(acc, row, m, n):
+    block = lambda i, j: acc[row + m * i : row + m * i + m, n * j : n * j + n]
     small = block(2, 2) + (block(1, 2) + block(2, 1))
     small = small + (block(0, 2) + block(2, 0)) + block(1, 1)
     return small + (block(0, 1) + block(1, 0)) + block(0, 0)
 
 
 def gram(first, second):
-    same, cross, last = merge_parts(first, 0), merge_parts(second, 0), merge_parts(second, 96)
+    m, n = 2 * SIZES[0], 2 * SIZES[1]
+    same, cross, last = merge_parts(first, 0, m, m), merge_parts(second, 0, m, n), merge_parts(second, 3 * m, n, n)
     g = jnp.concatenate(
         [jnp.concatenate([same, cross], axis=1), jnp.concatenate([cross.T, last], axis=1)], axis=0
     )
-    swap = lambda m, dim: jnp.concatenate(
-        [lax.slice_in_dim(m, at, at + 16, axis=dim) for at in (0, 32, 16, 48)], axis=dim
-    )
+    spans = ((0, m // 2), (m, m + n // 2), (m // 2, m), (m + n // 2, m + n))
+    swap = lambda v, dim: jnp.concatenate([lax.slice_in_dim(v, low, high, axis=dim) for low, high in spans], axis=dim)
     g = swap(swap(g, 0), 1)
     return jnp.concatenate([g[:32], g[32:]], axis=1)
 
@@ -240,29 +244,30 @@
 
 
 def unpack_part(part, back, mixed, scale):
-    left = iota((ROWS, LANES), 1) < 64
+    base, size = LOWS[part], SIZES[part]
+    left = iota((size, LANES), 1) < 64
 
     def step(i, carry):
-        for k in range(8):
-            b = 8 * i + k
+        for k in range(16):
+            b = 16 * i + k
             at = pl.ds(pl.multiple_of(b * 128, 128), 128)
-            one, two = back[2 * b, pl.ds(part * ROWS, ROWS)], back[2 * b + 1, pl.ds(part * ROWS, ROWS)]
+            one, two = back[2 * b, pl.ds(base, size)], back[2 * b + 1, pl.ds(base, size)]
             upper = jnp.where(left, one, pltpu.roll(two, 64, 1))
             lower = jnp.where(left, pltpu.roll(one, 64, 1), two)
-            mixed[part * ROWS : part * ROWS + ROWS, at] = upper * scale
-            mixed[HALF + part * ROWS : HALF + part * ROWS + ROWS, at] = lower * scale
-        return carry
-
-    lax.fori_loop(0, 8, step, 0)
+            mixed[base : base + size, at] = upper * scale
+            mixed[HALF + base : HALF + base + size, at] = lower * scale
+        return carry
+
+    lax.fori_loop(0, 4, step, 0)
 
 
 def pick_part(part, mixed, places, picked):
-    bases = [half + part * ROWS + 8 * k for half in (0, HALF) for k in range(ROWS // 8)]
+    bases = [half + LOWS[part] + 8 * k for half in (0, HALF) for k in range(SIZES[part] // 8)]
     for r, (high, low) in enumerate(places):
 
         def step(i, found):
-            for k in range(16):
-                b = 16 * i + k
+            for k in range(64):
+                b = 64 * i + k
                 at = pl.ds(pl.multiple_of(b * 128, 128), 128)
                 here = high == b
                 found = tuple(
@@ -275,7 +280,7 @@
                 )
             return found
 
-        done = lax.fori_loop(0, 4, step, tuple(jnp.zeros((8, LANES), F32) for _ in bases))
+        done = lax.fori_loop(0, 1, step, tuple(jnp.zeros((8, LANES), F32) for _ in bases))
         for base, value in zip(bases, done):
             picked[r, base : base + 8] = value
 
@@ -395,7 +400,7 @@
     signal_all(barrier, in_line, 8)
     signal_all(barrier, in_plane, 16)
     table[...] = lane_table()
-    rows = lambda part: pl.ds(part * ROWS, ROWS)
+    rows = lambda part: pl.ds(LOWS[part], SIZES[part])
 
     def send_out(part, groups):
         for group, low, high in groups:
@@ -420,7 +425,7 @@
     tables[0].wait()
     for part in range(PARTS):
         for g in range(8):
-            if (g % 4) * 8 // ROWS == part:
+            if 0 <= (g % 4) * 8 - LOWS[part] < SIZES[part]:
                 loads[g].wait()
         local_mix(part, panel, signs, table, send)
         if part == 0:
@@ -531,9 +536,9 @@
             pltpu.VMEM((DEVS, HALF, LANES), F32),
             pltpu.VMEM((DEVS, HALF, LANES), F32),
             pltpu.VMEM((64, 128), F32),
-            pltpu.VMEM((32, 96, 256), BF16),
-            pltpu.VMEM((96, 96), F32),
-            pltpu.VMEM((192, 96), F32),
+            pltpu.VMEM((32, 6 * SIZES[0], 256), BF16),
+            pltpu.VMEM((6 * SIZES[0], 6 * SIZES[0]), F32),
+            pltpu.VMEM((192, 6 * SIZES[1]), F32),
             pltpu.VMEM((8, 32, 128), F32),
             pltpu.VMEM((16, 32, 128), F32),
             pltpu.VMEM((CAP, 64, 128), F32),

time: 75.6 us -> 74.4 us (0.984)
  Pallas kernels: 74.9 us -> 73.7 us
    pallas_call x1, Pallas kernels: 73.5 us -> 72.2 us  [local(): pl.pallas_call(kernel, out_shape=(shape(64, 8192), shape(64, 64), shape(6...]
where the time goes in v5:
time: 74.4 us; the launch traced here: 74.3 us
  Pallas kernels  73.7 us (99%)
    pallas_call x1, Pallas kernels, local(): pl.pallas_call(kernel, out_shape=(shape(64, 8192), shape(64, 64), shape(6...  72.2 us

profile of v5, /device:TPU:1, one launch (start us, length us, event | category | flops | bytes accessed | tf_op | source)
XLA Modules:
  0.0 74.3 jit_solution(210345578792707481)
XLA Ops:
  0.6 72.2 %shard_map.67 = (f32[64,8192]{1,0:T(8,128)S(1)}, f32[64,64]{1,0:T(8,128)S(1)}, f32[64,128]{1,0:T(8,128)S(1)}) custom-call(f32[64,8192]{1,0:T(8,128)} %panel_hbm.1, s32[1,8192]{1,0:T(1,128)} %bitcast.5, s32[128,128]{1,0:T(8,128)} %bitcast.3, s32[128,128]{1,0:T(8,128)} %bitcast.4), custom_call_target="tpu_custom_call" | custom-call | tf_op jit(solution)/shard_map/pallas_call | solution.py:524
  72.9 1.4 %shard_map.68 = (f32[64,8192]{1,0:T(8,128)}, f32[64,64]{1,0:T(8,128)}, f32[64,128]{1,0:T(8,128)}) custom-call(f32[64,8192]{1,0:T(8,128)S(1)} %get-tuple-element.6.mixed_in, f32[64,64]{1,0:T(8,128)S(1)} %get-tuple-element.7.factor_in, f32[64,128]{1,0:T(8,128)S(1)} %get-tuple-element.8.whitened_in), custom_call_target="tpu_custom_call" | custom-call | tf_op jit(solution)/shard_map/pallas_call | solution.py:554
